TPU v7x, 32 devices: a whole 2x2x4 slice. The times are simulated.
32 devices in a mesh: gx: 2 (over x), gy: 4 (over y, core), gz: 4 (over z).
Axes of the slice: x: 2, y: 2, z: 4, core: 2. Of those that a mesh axis runs over, the one named last changes fastest.
Arguments:
- vectors: bfloat16 [2, 3, 8, 16, 16, 256], P(None, None, 'gx', 'gy', 'gz'), may hold values from -6 to 6
- gauge_links: float32 [3, 2, 3, 3, 8, 16, 16], P(None, None, None, None, 'gx', 'gy', 'gz'), may hold values from -2.5 to 2.5
- momenta: int32 [2, 3], replicated, may hold values from 1 to 3
- perambulator: bfloat16 [32, 2, 256, 4, 256], P(('gx', 'gy', 'gz')), may hold values from -0.19921875 to 0.19921875
Outputs:
- smeared: bfloat16 [2, 3, 8, 16, 16, 256], P(None, None, 'gx', 'gy', 'gz')
- sandwich: bfloat16 [32, 2, 2, 256, 256], P(('gx', 'gy', 'gz'))
All inputs are finite; a program needn't handle non-finite values.
Results may differ from a plain program's by a relative error of at most 0.0074.
Values may be sent and summed in bfloat16 or wider, within the bound.
A program may use at most 64 MiB of HBM per device.

v0:
```python
import math

import jax
import jax.numpy as jnp
from jax import lax
from jax.sharding import PartitionSpec as P


def passed_along(value, axis, steps):
    count = lax.axis_size(axis)
    pairs = [(source, (source + steps) % count) for source in range(count)]
    return lax.ppermute(value, axis, pairs)


def padded_2(cells, sides, width):
    for axis, dim in sides:
        count = lax.axis_size(axis)
        head = lax.slice_in_dim(cells, 0, width, axis=dim)
        tail = lax.slice_in_dim(cells, cells.shape[dim] - width, cells.shape[dim], axis=dim)
        cells = jnp.concatenate(
            [
                lax.ppermute(tail, axis, [(i, (i + 1) % count) for i in range(count)]),
                cells,
                lax.ppermute(head, axis, [((i + 1) % count, i) for i in range(count)]),
            ],
            axis=dim,
        )
    return cells


def link_times(link_mu, colour_field, adjoint):
    real_part = None
    imag_part = None
    for column in range(3):
        if adjoint:
            link_real = link_mu[0][column]
            link_imag = -link_mu[1][column]
        else:
            link_real = link_mu[0][:, column]
            link_imag = link_mu[1][:, column]
        link_real = link_real[..., None]
        link_imag = link_imag[..., None]
        field_real = colour_field[0][column]
        field_imag = colour_field[1][column]
        add_real = link_real * field_real - link_imag * field_imag
        add_imag = link_real * field_imag + link_imag * field_real
        real_part = add_real if real_part is None else real_part + add_real
        imag_part = add_imag if imag_part is None else imag_part + add_imag
    return jnp.stack([real_part, imag_part])


def phase_tables(momenta, pos_x, pos_y, pos_z, cells_x, cells_y, cells_z):
    frac_x = (momenta[:, 0:1] * pos_x[None, :] % cells_x).astype(jnp.float32) / cells_x
    frac_y = (momenta[:, 1:2] * pos_y[None, :] % cells_y).astype(jnp.float32) / cells_y
    frac_z = (momenta[:, 2:3] * pos_z[None, :] % cells_z).astype(jnp.float32) / cells_z
    lattice_fraction = (
        frac_x[:, :, None, None] + frac_y[:, None, :, None] + frac_z[:, None, None, :]
    )
    theta = 2.0 * math.pi * lattice_fraction
    return (jnp.cos(theta), jnp.sin(theta))


def per_device(vectors, gauge_links, momenta, perambulator):
    size_x = vectors.shape[2]
    size_y = vectors.shape[3]
    size_z = vectors.shape[4]
    width = vectors.shape[5]
    moms = momenta.shape[0]
    link_x = gauge_links[0]
    ghost_x = passed_along(link_x[:, :, :, size_x - 1 :, :, :], "gx", 1)
    below_x = jnp.concatenate([ghost_x, link_x[:, :, :, : size_x - 1, :, :]], axis=3)
    link_y = gauge_links[1]
    ghost_y = passed_along(link_y[:, :, :, :, size_y - 1 :, :], "gy", 1)
    below_y = jnp.concatenate([ghost_y, link_y[:, :, :, :, : size_y - 1, :]], axis=4)
    link_z = gauge_links[2]
    ghost_z = passed_along(link_z[:, :, :, :, :, size_z - 1 :], "gz", 1)
    below_z = jnp.concatenate([ghost_z, link_z[:, :, :, :, :, : size_z - 1]], axis=5)
    links_here = (link_x, link_y, link_z)
    links_below = (below_x, below_y, below_z)

    def neighbour_sum(colour_field):
        padded = padded_2(colour_field, (("gx", 2), ("gy", 3), ("gz", 4)), 1)
        upper_neighbours = (
            padded[:, :, 2:, 1:-1, 1:-1],
            padded[:, :, 1:-1, 2:, 1:-1],
            padded[:, :, 1:-1, 1:-1, 2:],
        )
        belows = (
            padded[:, :, :-2, 1:-1, 1:-1],
            padded[:, :, 1:-1, :-2, 1:-1],
            padded[:, :, 1:-1, 1:-1, :-2],
        )
        summed = None
        for axis_mu in range(3):
            hop_term = link_times(
                links_here[axis_mu], upper_neighbours[axis_mu], False
            ) + link_times(links_below[axis_mu], belows[axis_mu], True)
            summed = hop_term if summed is None else summed + hop_term
        return summed

    initial_recursion = (neighbour_sum(vectors) / 6.0).astype(jnp.bfloat16)
    second = neighbour_sum(initial_recursion)
    smeared = (2.0 * second / 6.0 - vectors.astype(jnp.float32)).astype(jnp.bfloat16)
    cells_x = size_x * lax.axis_size("gx")
    cells_y = size_y * lax.axis_size("gy")
    cells_z = size_z * lax.axis_size("gz")
    pos_x = lax.axis_index("gx") * size_x + jnp.arange(size_x, dtype=jnp.int32)
    pos_y = lax.axis_index("gy") * size_y + jnp.arange(size_y, dtype=jnp.int32)
    pos_z = lax.axis_index("gz") * size_z + jnp.arange(size_z, dtype=jnp.int32)
    cos_table, sin_table = phase_tables(momenta, pos_x, pos_y, pos_z, cells_x, cells_y, cells_z)
    sites = size_x * size_y * size_z
    cos_b = cos_table.reshape(moms, 1, sites, 1)
    sin_b = sin_table.reshape(moms, 1, sites, 1)
    smeared_flat = smeared.reshape(2, 3, sites, width)
    real_w = smeared_flat[0].astype(jnp.float32)[None]
    imag_w = smeared_flat[1].astype(jnp.float32)[None]
    real_z = (cos_b * real_w + sin_b * imag_w).astype(jnp.bfloat16)
    imag_z = (cos_b * imag_w - sin_b * real_w).astype(jnp.bfloat16)
    left_rows = smeared_flat.reshape(6 * sites, width)
    right_real = jnp.concatenate([real_z, imag_z], axis=1).reshape(moms, 6 * sites, width)
    right_imag = jnp.concatenate([imag_z, -real_z], axis=1).reshape(moms, 6 * sites, width)
    right_both = jnp.stack([right_real, right_imag], 0)
    norm_scale = 1.0 / math.sqrt(3.0 * cells_x * cells_y * cells_z)
    partial_terms = (
        jnp.einsum("cmrb,ra->cmba", right_both, left_rows, preferred_element_type=jnp.float32)
        * norm_scale
    )
    elemental_rows = partial_terms.reshape(2 * moms * width, width)
    gathered = lax.psum(elemental_rows, ("gx", "gy", "gz")).astype(jnp.bfloat16)
    elementals_low = gathered.reshape(2, moms, width, width)
    count = perambulator.shape[0]
    spins = perambulator.shape[3]
    cols = perambulator.shape[4]
    elem_real = elementals_low[0]
    elem_imag = elementals_low[1]
    multiplier_real = jnp.concatenate([elem_real, elem_imag], axis=2)
    multiplier_imag = jnp.concatenate([elem_imag, -elem_real], axis=2)
    factor_both = jnp.stack([multiplier_real, multiplier_imag], 1)
    peram_rows = perambulator.reshape(count, 2 * width, spins * cols)
    inner = jnp.einsum(
        "mcbq,nqk->nmcbk", factor_both, peram_rows, preferred_element_type=jnp.float32
    ).astype(jnp.bfloat16)
    inner_rows = inner.reshape(count, moms, 2, width * spins, cols)
    peram_parts = perambulator.reshape(count, 2, width * spins, cols)
    pairwise_products = jnp.einsum(
        "nmcrk,ndrl->nmcdkl", inner_rows, peram_parts, preferred_element_type=jnp.float32
    )
    sandwich_real = pairwise_products[:, :, 0, 0] - pairwise_products[:, :, 1, 1]
    sandwich_imag = pairwise_products[:, :, 0, 1] + pairwise_products[:, :, 1, 0]
    sandwich = jnp.stack([sandwich_real, sandwich_imag], 2).astype(jnp.bfloat16)
    return (smeared, sandwich)


def solution(mesh):
    return jax.shard_map(
        per_device,
        mesh=mesh,
        in_specs=(
            P(None, None, "gx", "gy", "gz", None),
            P(None, None, None, None, "gx", "gy", "gz"),
            P(),
            P(("gx", "gy", "gz"), None, None, None, None),
        ),
        out_specs=(
            P(None, None, "gx", "gy", "gz", None),
            P(("gx", "gy", "gz"), None, None, None, None),
        ),
        check_vma=False,
    )
```

profile of v0, /device:TPU:0, one launch (start us, length us, event | category | flops | bytes accessed | tf_op | source)
XLA Modules:
  0.0 124.8 jit_solution(7040163077360449852)
XLA Ops:
  0.6 0.9 fusion.171
  1.5 3.0 %collective-permute-start.2 = (bf16[2,3,1,4,4,256]{5,4,3,2,1,0:T(4,128)(2,1)S(1)}, bf16[2,3,1,4,4,256]{5,4,3,2,1,0:T(4,128)(2,1)S(1)}, u32[]{:S(2)}, u32[]{:S(2)}) collective-permute-start(bf16[2,3,1,4,4,256]{5,4,3,2,1,0:T(4,128)(2,1)S(1)} %get-tuple-element.159), channel_id=1, source_target_pairs={{0,16},{16,0},{1,17},{17,1},{2,18},{18,2},{3,19},{19,3},{4,20},{20... | collective-permute-start | bytes 147464 | tf_op jit(solution)/shard_map/ppermute | solution.py:22
  4.6 1.1 slice_bitcast_fusion.2
  5.8 2.0 %collective-permute-start.1 = (f32[2,3,3,1,4,4]{5,4,3,2,1,0:T(4,128)S(1)}, f32[2,3,3,1,4,4]{5,4,3,2,1,0:T(4,128)S(1)}, u32[]{:S(2)}, u32[]{:S(2)}) collective-permute-start(f32[2,3,3,1,4,4]{5,4,3,2,1,0:T(4,128)S(1)} %slice.1017), channel_id=1, source_target_pairs={{0,16},{16,0},{1,17},{17,1},{2,18},{18,2},{3,19},{19,3},{4,20},{20... | collective-permute-start | bytes 3464 | tf_op jit(solution)/shard_map/ppermute | solution.py:12
  8.0 1.6 %collective-permute-start.7 = (f32[2,3,3,4,4,1]{5,4,3,2,1,0:T(4,128)S(1)}, f32[2,3,3,4,4,1]{5,4,3,2,1,0:T(4,128)S(1)}, u32[]{:S(2)}, u32[]{:S(2)}) collective-permute-start(f32[2,3,3,4,4,1]{5,4,3,2,1,0:T(4,128)S(1)} %slice.1062), channel_id=1, source_target_pairs={{0,1},{1,2},{2,3},{3,0},{4,5},{5,6},{6,7},{7,4},{8,9},{9,10},{10,1... | collective-permute-start | bytes 3464 | tf_op jit(solution)/shard_map/ppermute | solution.py:12
  9.6 1.1 slice_bitcast_fusion.6
  11.4 4.4 %collective-permute-done.7 = f32[2,3,3,4,4,1]{5,4,3,2,1,0:T(4,128)S(1)} collective-permute-done((f32[2,3,3,4,4,1]{5,4,3,2,1,0:T(4,128)S(1)}, f32[2,3,3,4,4,1]{5,4,3,2,1,0:T(4,128)S(1)}, u32[]{:S(2)}, u32[]{:S(2)}) %collective-permute-start.7) | collective-permute-done | bytes 1184 | tf_op jit(solution)/shard_map/ppermute | solution.py:12
  16.5 0.6 collective-permute-start.5
  17.1 1.2 collective-permute-start.3
  19.1 1.2 collective-permute-done.5
  21.2 3.8 %collective-permute-start.6 = (bf16[2,3,6,6,1,256]{5,4,3,2,1,0:T(2,128)(2,1)S(1)}, bf16[2,3,6,6,1,256]{5,4,3,2,1,0:T(2,128)(2,1)S(1)}, u32[]{:S(2)}, u32[]{:S(2)}) collective-permute-start(bf16[2,3,6,6,1,256]{5,4,3,2,1,0:T(2,128)(2,1)S(1)} %get-tuple-element.69), channel_id=1, source_target_pairs={{1,0},{2,1},{3,2},{0,3},{5,4},{6,5},{7,6},{4,7},{9,8},{10,9},{11,1... | collective-permute-start | bytes 331784 | tf_op jit(solution)/shard_map/ppermute | solution.py:24
  25.6 5.0 %collective-permute-done.8 = bf16[2,3,6,6,1,256]{5,4,3,2,1,0:T(2,128)(2,1)S(1)} collective-permute-done((bf16[2,3,6,6,1,256]{5,4,3,2,1,0:T(2,128)(2,1)S(1)}, bf16[2,3,6,6,1,256]{5,4,3,2,1,0:T(2,128)(2,1)S(1)}, u32[]{:S(2)}, u32[]{:S(2)}) %collective-permute-start.8) | collective-permute-done | bytes 110624 | tf_op jit(solution)/shard_map/ppermute | solution.py:22
  30.7 2.8 %collective-permute-done.6 = bf16[2,3,6,6,1,256]{5,4,3,2,1,0:T(2,128)(2,1)S(1)} collective-permute-done((bf16[2,3,6,6,1,256]{5,4,3,2,1,0:T(2,128)(2,1)S(1)}, bf16[2,3,6,6,1,256]{5,4,3,2,1,0:T(2,128)(2,1)S(1)}, u32[]{:S(2)}, u32[]{:S(2)}) %collective-permute-start.6) | collective-permute-done | bytes 110624 | tf_op jit(solution)/shard_map/ppermute | solution.py:24
  35.6 0.7 fusion.170
  36.8 1.4 %collective-permute-start.9 = (bf16[2,3,1,4,4,256]{5,4,3,2,1,0:T(4,128)(2,1)S(1)}, bf16[2,3,1,4,4,256]{5,4,3,2,1,0:T(4,128)(2,1)S(1)}, u32[]{:S(2)}, u32[]{:S(2)}) collective-permute-start(bf16[2,3,1,4,4,256]{5,4,3,2,1,0:T(4,128)(2,1)S(1)} %get-tuple-element.155), channel_id=1, source_target_pairs={{16,0},{0,16},{17,1},{1,17},{18,2},{2,18},{19,3},{3,19},{20,4},{4,... | collective-permute-start | bytes 147464 | tf_op jit(solution)/shard_map/ppermute | solution.py:24
  38.8 1.6 %reshape.1965 = bf16[512,1024,1,1]{1,0,2,3:T(8,128)(2,1)} reshape(bf16[1,2,256,4,256]{4,3,2,1,0:T(4,128)(2,1)S(1)} %copy-done) | data formatting | bytes 2097152 | tf_op jit(solution)/shard_map/reshape.212
  41.1 0.7 collective-permute-done.9
  42.0 1.7 %collective-permute-start.11 = (bf16[2,3,6,1,4,256]{5,4,3,2,1,0:T(4,128)(2,1)S(1)}, bf16[2,3,6,1,4,256]{5,4,3,2,1,0:T(4,128)(2,1)S(1)}, u32[]{:S(2)}, u32[]{:S(2)}) collective-permute-start(bf16[2,3,6,1,4,256]{5,4,3,2,1,0:T(4,128)(2,1)S(1)} %get-tuple-element.103), channel_id=1, source_target_pairs={{4,0},{8,4},{12,8},{0,12},{5,1},{9,5},{13,9},{1,13},{6,2},{10,6},{... | collective-permute-start | bytes 221192 | tf_op jit(solution)/shard_map/ppermute | solution.py:24
  44.3 1.5 %collective-permute-done.12 = bf16[2,3,6,1,4,256]{5,4,3,2,1,0:T(4,128)(2,1)S(1)} collective-permute-done((bf16[2,3,6,1,4,256]{5,4,3,2,1,0:T(4,128)(2,1)S(1)}, bf16[2,3,6,1,4,256]{5,4,3,2,1,0:T(4,128)(2,1)S(1)}, u32[]{:S(2)}, u32[]{:S(2)}) %collective-permute-start.12) | collective-permute-done | bytes 73760 | tf_op jit(solution)/shard_map/ppermute | solution.py:22
  46.4 1.3 %collective-permute-start.14 = (bf16[2,3,6,6,1,256]{5,4,3,2,1,0:T(2,128)(2,1)S(1)}, bf16[2,3,6,6,1,256]{5,4,3,2,1,0:T(2,128)(2,1)S(1)}, u32[]{:S(2)}, u32[]{:S(2)}) collective-permute-start(bf16[2,3,6,6,1,256]{5,4,3,2,1,0:T(2,128)(2,1)S(1)} %get-tuple-element.61), channel_id=1, source_target_pairs={{0,1},{1,2},{2,3},{3,0},{4,5},{5,6},{6,7},{7,4},{8,9},{9,10},{10,1... | collective-permute-start | bytes 331784 | tf_op jit(solution)/shard_map/ppermute | solution.py:22
  47.7 2.6 %collective-permute-start.13 = (bf16[2,3,6,6,1,256]{5,4,3,2,1,0:T(2,128)(2,1)S(1)}, bf16[2,3,6,6,1,256]{5,4,3,2,1,0:T(2,128)(2,1)S(1)}, u32[]{:S(2)}, u32[]{:S(2)}) collective-permute-start(bf16[2,3,6,6,1,256]{5,4,3,2,1,0:T(2,128)(2,1)S(1)} %get-tuple-element.62), channel_id=1, source_target_pairs={{1,0},{2,1},{3,2},{0,3},{5,4},{6,5},{7,6},{4,7},{9,8},{10,9},{11,1... | collective-permute-start | bytes 331784 | tf_op jit(solution)/shard_map/ppermute | solution.py:24
  51.8 4.3 %collective-permute-done.14 = bf16[2,3,6,6,1,256]{5,4,3,2,1,0:T(2,128)(2,1)S(1)} collective-permute-done((bf16[2,3,6,6,1,256]{5,4,3,2,1,0:T(2,128)(2,1)S(1)}, bf16[2,3,6,6,1,256]{5,4,3,2,1,0:T(2,128)(2,1)S(1)}, u32[]{:S(2)}, u32[]{:S(2)}) %collective-permute-start.14) | collective-permute-done | bytes 110624 | tf_op jit(solution)/shard_map/ppermute | solution.py:22
  56.7 3.8 %collective-permute-done.13 = bf16[2,3,6,6,1,256]{5,4,3,2,1,0:T(2,128)(2,1)S(1)} collective-permute-done((bf16[2,3,6,6,1,256]{5,4,3,2,1,0:T(2,128)(2,1)S(1)}, bf16[2,3,6,6,1,256]{5,4,3,2,1,0:T(2,128)(2,1)S(1)}, u32[]{:S(2)}, u32[]{:S(2)}) %collective-permute-start.13) | collective-permute-done | bytes 110624 | tf_op jit(solution)/shard_map/ppermute | solution.py:24
  61.1 0.6 fusion.24
  62.6 0.9 copy.14
  63.6 1.4 %convolution_multiply_fusion = f32[2,2,256,256]{3,2,1,0:T(8,128)S(1)} fusion(bf16[1,2,384,256]{2,3,1,0:T(8,128)(2,1)} %copy.14, bf16[1,2,384,256]{2,3,1,0:T(8,128)(2,1)S(1)} %copy.13, bf16[384,256,1,1]{1,0,2,3:T(8,128)(2,1)S(1)} %reshape.1964), kind=kOutput, calls=%fused_computation.4 | convolution fusion | flops 201981952 | bytes 2031616 | tf_op jit(solution)/shard_map/cmrb,ra->cmba/dot_general | solution.py:125
  65.0 50.9 %all-reduce.1 = bf16[1024,256]{1,0:T(8,128)(2,1)S(1)} all-reduce(f32[1024,256]{1,0:T(8,128)S(1)} %bitcast.516), channel_id=1, replica_groups=mesh['gx'=2,'gy'=4,'gz'=4] {'gx','gy','gz'}, use_global_device_ids=true, to_apply=%region_0.1 | all-reduce | flops 262144 | bytes 1572864 | tf_op jit(solution)/shard_map/psum | solution.py:129
  116.0 1.0 copy-done.3
  117.1 1.3 %convert_bitcast_fusion = bf16[1,2,2,256,1024]{4,3,2,1,0:T(8,128)(2,1)S(1)} fusion(bf16[2,1,256,512]{3,2,1,0:T(8,128)(2,1)S(1)} %get-tuple-element.119, bf16[2,1,256,512]{3,2,1,0:T(8,128)(2,1)S(1)} %get-tuple-element.118, bf16[512,1024,1,1]{1,0,2,3:T(8,128)(2,1)S(1)} %copy-done.3), kind=kOutput, calls=%fused_computation.2 | convolution fusion | flops 1075314688 | bytes 4194304 | tf_op jit(solution)/shard_map/mcbq,nqk->nmcbk/dot_general | solution.py:140
  118.3 2.6 %reshape.1888 = bf16[2,2,1024,256]{3,2,1,0:T(8,128)(2,1)} reshape(bf16[1,2,2,256,1024]{4,3,2,1,0:T(8,128)(2,1)S(1)} %convert_bitcast_fusion) | data formatting | bytes 4194304 | tf_op jit(solution)/shard_map/reshape.215
  120.9 2.9 %fusion.2 = f32[1,2,2,2,256,256]{5,4,3,2,1,0:T(8,128)S(1)} fusion(bf16[2,2,1024,256]{3,2,1,0:T(8,128)(2,1)} %reshape.1888, bf16[2,1024,256,1,1]{2,1,0,3,4:T(8,128)(2,1)S(1)} %reshape.1967), kind=kOutput, calls=%fused_computation.3 | convolution fusion | flops 1073741824 | bytes 5242880 | tf_op jit(solution)/shard_map/nmcrk,ndrl->nmcdkl/dot_general | solution.py:145
  124.0 0.8 copy.19
  (92 shorter events, 13.0 us)
Async XLA Ops:
  0.6 10.1 %copy-start.4 = (s32[2,3]{1,0:T(2,128)S(1)}, s32[2,3]{1,0:T(2,128)}, u32[]{:S(2)}) copy-start(s32[2,3]{1,0:T(2,128)} %param.6) | copy-start | bytes 76
  1.5 14.5 %collective-permute-start.2 = (bf16[2,3,1,4,4,256]{5,4,3,2,1,0:T(4,128)(2,1)S(1)}, bf16[2,3,1,4,4,256]{5,4,3,2,1,0:T(4,128)(2,1)S(1)}, u32[]{:S(2)}, u32[]{:S(2)}) collective-permute-start(bf16[2,3,1,4,4,256]{5,4,3,2,1,0:T(4,128)(2,1)S(1)} %get-tuple-element.159), channel_id=1, source_target_pairs={{0,16},{16,0},{1,17},{17,1},{2,18},{18,2},{3,19},{19,3},{4,20},{20... | collective-permute-start | bytes 147464 | tf_op jit(solution)/shard_map/ppermute | solution.py:22
  4.5 11.5 %copy-start.2 = (bf16[2,3,4,4,4,256]{5,4,3,2,1,0:T(4,128)(2,1)S(1)}, bf16[2,3,4,4,4,256]{5,4,3,2,1,0:T(4,128)(2,1)}, u32[]{:S(2)}) copy-start(bf16[2,3,4,4,4,256]{5,4,3,2,1,0:T(4,128)(2,1)} %param.4) | copy-start | bytes 589828
  4.5 11.8 %collective-permute-start = (bf16[2,3,1,4,4,256]{5,4,3,2,1,0:T(4,128)(2,1)S(1)}, bf16[2,3,1,4,4,256]{5,4,3,2,1,0:T(4,128)(2,1)S(1)}, u32[]{:S(2)}, u32[]{:S(2)}) collective-permute-start(bf16[2,3,1,4,4,256]{5,4,3,2,1,0:T(4,128)(2,1)S(1)} %get-tuple-element.160), channel_id=1, source_target_pairs={{16,0},{0,16},{17,1},{1,17},{18,2},{2,18},{19,3},{3,19},{20,4},{4,... | collective-permute-start | bytes 147464 | tf_op jit(solution)/shard_map/ppermute | solution.py:24
  5.8 5.5 %collective-permute-start.1 = (f32[2,3,3,1,4,4]{5,4,3,2,1,0:T(4,128)S(1)}, f32[2,3,3,1,4,4]{5,4,3,2,1,0:T(4,128)S(1)}, u32[]{:S(2)}, u32[]{:S(2)}) collective-permute-start(f32[2,3,3,1,4,4]{5,4,3,2,1,0:T(4,128)S(1)} %slice.1017), channel_id=1, source_target_pairs={{0,16},{16,0},{1,17},{17,1},{2,18},{18,2},{3,19},{19,3},{4,20},{20... | collective-permute-start | bytes 3464 | tf_op jit(solution)/shard_map/ppermute | solution.py:12
  7.8 3.6 %collective-permute-start.4 = (f32[2,3,3,4,1,4]{5,4,3,2,1,0:T(1,128)S(1)}, f32[2,3,3,4,1,4]{5,4,3,2,1,0:T(1,128)S(1)}, u32[]{:S(2)}, u32[]{:S(2)}) collective-permute-start(f32[2,3,3,4,1,4]{5,4,3,2,1,0:T(1,128)S(1)} %slice.1042), channel_id=1, source_target_pairs={{0,4},{4,8},{8,12},{12,0},{1,5},{5,9},{9,13},{13,1},{2,6},{6,10},{... | collective-permute-start | bytes 3464 | tf_op jit(solution)/shard_map/ppermute | solution.py:12
  8.0 7.9 %collective-permute-start.7 = (f32[2,3,3,4,4,1]{5,4,3,2,1,0:T(4,128)S(1)}, f32[2,3,3,4,4,1]{5,4,3,2,1,0:T(4,128)S(1)}, u32[]{:S(2)}, u32[]{:S(2)}) collective-permute-start(f32[2,3,3,4,4,1]{5,4,3,2,1,0:T(4,128)S(1)} %slice.1062), channel_id=1, source_target_pairs={{0,1},{1,2},{2,3},{3,0},{4,5},{5,6},{6,7},{7,4},{8,9},{9,10},{10,1... | collective-permute-start | bytes 3464 | tf_op jit(solution)/shard_map/ppermute | solution.py:12
  16.5 3.8 %collective-permute-start.5 = (bf16[2,3,6,1,4,256]{5,4,3,2,1,0:T(4,128)(2,1)S(1)}, bf16[2,3,6,1,4,256]{5,4,3,2,1,0:T(4,128)(2,1)S(1)}, u32[]{:S(2)}, u32[]{:S(2)}) collective-permute-start(bf16[2,3,6,1,4,256]{5,4,3,2,1,0:T(4,128)(2,1)S(1)} %get-tuple-element.116), channel_id=1, source_target_pairs={{0,4},{4,8},{8,12},{12,0},{1,5},{5,9},{9,13},{13,1},{2,6},{6,10},{... | collective-permute-start | bytes 221192 | tf_op jit(solution)/shard_map/ppermute | solution.py:22
  17.1 3.5 %collective-permute-start.3 = (bf16[2,3,6,1,4,256]{5,4,3,2,1,0:T(4,128)(2,1)S(1)}, bf16[2,3,6,1,4,256]{5,4,3,2,1,0:T(4,128)(2,1)S(1)}, u32[]{:S(2)}, u32[]{:S(2)}) collective-permute-start(bf16[2,3,6,1,4,256]{5,4,3,2,1,0:T(4,128)(2,1)S(1)} %get-tuple-element.117), channel_id=1, source_target_pairs={{4,0},{8,4},{12,8},{0,12},{5,1},{9,5},{13,9},{1,13},{6,2},{10,6},{... | collective-permute-start | bytes 221192 | tf_op jit(solution)/shard_map/ppermute | solution.py:24
  21.2 9.4 %collective-permute-start.8 = (bf16[2,3,6,6,1,256]{5,4,3,2,1,0:T(2,128)(2,1)S(1)}, bf16[2,3,6,6,1,256]{5,4,3,2,1,0:T(2,128)(2,1)S(1)}, u32[]{:S(2)}, u32[]{:S(2)}) collective-permute-start(bf16[2,3,6,6,1,256]{5,4,3,2,1,0:T(2,128)(2,1)S(1)} %get-tuple-element.68), channel_id=1, source_target_pairs={{0,1},{1,2},{2,3},{3,0},{4,5},{5,6},{6,7},{7,4},{8,9},{9,10},{10,1... | collective-permute-start | bytes 331784 | tf_op jit(solution)/shard_map/ppermute | solution.py:22
  21.2 12.3 %collective-permute-start.6 = (bf16[2,3,6,6,1,256]{5,4,3,2,1,0:T(2,128)(2,1)S(1)}, bf16[2,3,6,6,1,256]{5,4,3,2,1,0:T(2,128)(2,1)S(1)}, u32[]{:S(2)}, u32[]{:S(2)}) collective-permute-start(bf16[2,3,6,6,1,256]{5,4,3,2,1,0:T(2,128)(2,1)S(1)} %get-tuple-element.69), channel_id=1, source_target_pairs={{1,0},{2,1},{3,2},{0,3},{5,4},{6,5},{7,6},{4,7},{9,8},{10,9},{11,1... | collective-permute-start | bytes 331784 | tf_op jit(solution)/shard_map/ppermute | solution.py:24
  34.6 3.9 %copy-start = (bf16[1,2,256,4,256]{4,3,2,1,0:T(4,128)(2,1)S(1)}, bf16[1,2,256,4,256]{4,3,2,1,0:T(4,128)(2,1)}, u32[]{:S(2)}) copy-start(bf16[1,2,256,4,256]{4,3,2,1,0:T(4,128)(2,1)} %param.7) | copy-start | bytes 3145732
  36.3 4.8 %collective-permute-start.10 = (bf16[2,3,1,4,4,256]{5,4,3,2,1,0:T(4,128)(2,1)}, bf16[2,3,1,4,4,256]{5,4,3,2,1,0:T(4,128)(2,1)S(1)}, u32[]{:S(2)}, u32[]{:S(2)}) collective-permute-start(bf16[2,3,1,4,4,256]{5,4,3,2,1,0:T(4,128)(2,1)} %get-tuple-element.154), channel_id=1, source_target_pairs={{0,16},{16,0},{1,17},{17,1},{2,18},{18,2},{3,19},{19,3},{4,20},{20... | collective-permute-start | bytes 147464 | tf_op jit(solution)/shard_map/ppermute | solution.py:22
  36.8 5.0 %collective-permute-start.9 = (bf16[2,3,1,4,4,256]{5,4,3,2,1,0:T(4,128)(2,1)S(1)}, bf16[2,3,1,4,4,256]{5,4,3,2,1,0:T(4,128)(2,1)S(1)}, u32[]{:S(2)}, u32[]{:S(2)}) collective-permute-start(bf16[2,3,1,4,4,256]{5,4,3,2,1,0:T(4,128)(2,1)S(1)} %get-tuple-element.155), channel_id=1, source_target_pairs={{16,0},{0,16},{17,1},{1,17},{18,2},{2,18},{19,3},{3,19},{20,4},{4,... | collective-permute-start | bytes 147464 | tf_op jit(solution)/shard_map/ppermute | solution.py:24
  41.9 3.8 %collective-permute-start.12 = (bf16[2,3,6,1,4,256]{5,4,3,2,1,0:T(4,128)(2,1)S(1)}, bf16[2,3,6,1,4,256]{5,4,3,2,1,0:T(4,128)(2,1)S(1)}, u32[]{:S(2)}, u32[]{:S(2)}) collective-permute-start(bf16[2,3,6,1,4,256]{5,4,3,2,1,0:T(4,128)(2,1)S(1)} %get-tuple-element.102), channel_id=1, source_target_pairs={{0,4},{4,8},{8,12},{12,0},{1,5},{5,9},{9,13},{13,1},{2,6},{6,10},{... | collective-permute-start | bytes 221192 | tf_op jit(solution)/shard_map/ppermute | solution.py:22
  42.0 3.8 %collective-permute-start.11 = (bf16[2,3,6,1,4,256]{5,4,3,2,1,0:T(4,128)(2,1)S(1)}, bf16[2,3,6,1,4,256]{5,4,3,2,1,0:T(4,128)(2,1)S(1)}, u32[]{:S(2)}, u32[]{:S(2)}) collective-permute-start(bf16[2,3,6,1,4,256]{5,4,3,2,1,0:T(4,128)(2,1)S(1)} %get-tuple-element.103), channel_id=1, source_target_pairs={{4,0},{8,4},{12,8},{0,12},{5,1},{9,5},{13,9},{1,13},{6,2},{10,6},{... | collective-permute-start | bytes 221192 | tf_op jit(solution)/shard_map/ppermute | solution.py:24
  46.4 9.7 %collective-permute-start.14 = (bf16[2,3,6,6,1,256]{5,4,3,2,1,0:T(2,128)(2,1)S(1)}, bf16[2,3,6,6,1,256]{5,4,3,2,1,0:T(2,128)(2,1)S(1)}, u32[]{:S(2)}, u32[]{:S(2)}) collective-permute-start(bf16[2,3,6,6,1,256]{5,4,3,2,1,0:T(2,128)(2,1)S(1)} %get-tuple-element.61), channel_id=1, source_target_pairs={{0,1},{1,2},{2,3},{3,0},{4,5},{5,6},{6,7},{7,4},{8,9},{9,10},{10,1... | collective-permute-start | bytes 331784 | tf_op jit(solution)/shard_map/ppermute | solution.py:22
  47.7 12.8 %collective-permute-start.13 = (bf16[2,3,6,6,1,256]{5,4,3,2,1,0:T(2,128)(2,1)S(1)}, bf16[2,3,6,6,1,256]{5,4,3,2,1,0:T(2,128)(2,1)S(1)}, u32[]{:S(2)}, u32[]{:S(2)}) collective-permute-start(bf16[2,3,6,6,1,256]{5,4,3,2,1,0:T(2,128)(2,1)S(1)} %get-tuple-element.62), channel_id=1, source_target_pairs={{1,0},{2,1},{3,2},{0,3},{5,4},{6,5},{7,6},{4,7},{9,8},{10,9},{11,1... | collective-permute-start | bytes 331784 | tf_op jit(solution)/shard_map/ppermute | solution.py:24
  61.7 0.7 copy-start.1
  115.8 1.2 copy-start.3
where the time goes:
time: 125 us
  blocking collectives  50.9 us (41%)
  waiting for transfers between devices  24.4 us (20%)
  starting transfers between devices  20.1 us (16%)
  local copies, waits for them, and re-layouts  13.1 us (10%)
  other arithmetic  9.53 us (8%)
  matrix products  5.53 us (4%)
  between operations  1.25 us (1%)
    psum x1, blocking collectives, per_device(): gathered = lax.psum(elemental_rows, ('gx', 'gy', 'gz')).astype(jnp.bfloat16)  50.9 us
    ppermute x6, waiting for transfers between devices, padded_2(): lax.ppermute(tail, axis, [(i, (i + 1) % count) for i in range(count)])  12.5 us
    ppermute x6, starting transfers between devices, padded_2(): lax.ppermute(head, axis, [((i + 1) % count, i) for i in range(count)])  10.9 us
    ppermute x6, waiting for transfers between devices, padded_2(): lax.ppermute(head, axis, [((i + 1) % count, i) for i in range(count)])  7.56 us
    ppermute x6, starting transfers between devices, padded_2(): lax.ppermute(tail, axis, [(i, (i + 1) % count) for i in range(count)])  5.6 us
    add x12, other arithmetic, link_times(): real_part = add_real if real_part is None else real_part + add_real  4.6 us
    another operation x3, local copies, waits for them, and re-layouts  4.42 us
    ppermute x3, waiting for transfers between devices, passed_along(): return lax.ppermute(value, axis, pairs)  4.4 us
  transfers between devices with their start and end apart: 15, of which 10 were waited for; matrix products, arithmetic and copies ran while one was open for 8% of the time, Pallas kernels for 0%

commit v1 on v0

v1 whole, which is shorter than its diff:
```python
import functools
import math

import jax
import jax.numpy as jnp
import numpy as np
from jax import lax
from jax.experimental import pallas as pl
from jax.experimental.pallas import tpu as pltpu
from jax.sharding import PartitionSpec as P

AXES = ("gx", "gy", "gz")
MESH = pl.DeviceIdType.MESH
F32 = jnp.float32
BF16 = jnp.bfloat16


class Plan:
    def __init__(self, dims):
        self.dims = dims
        self.sites = int(np.prod(dims))
        grid = np.indices(dims).reshape(3, -1)
        strides = (dims[1] * dims[2], dims[2], 1)
        self.face = [self.sites // dims[mu] for mu in range(3)]
        offset, self.slot = 0, []
        for mu in range(3):
            for _ in range(2):
                self.slot.append(offset)
                offset += self.face[mu]
        self.halo = offset
        self.cols = -(-(self.sites + offset) // 128) * 128
        offset, self.ghost = 0, []
        for mu in range(3):
            self.ghost.append(offset)
            offset += self.face[mu]
        self.ghosts = offset
        self.link_rows = -(-(self.sites + offset) // 16) * 16
        code = np.zeros((self.sites, self.cols), np.int32)
        pick = np.zeros((self.halo, self.sites), np.float32)
        pick_link = np.zeros((self.ghosts, self.sites), np.float32)
        below = np.zeros((3 * self.sites, self.link_rows), np.float32)
        for mu in range(3):
            others = [a for a in range(3) if a != mu]
            for s in range(self.sites):
                at = grid[:, s]
                f = at[others[0]] * dims[others[1]] + at[others[1]]
                if at[mu] == dims[mu] - 1:
                    code[s, self.sites + self.slot[2 * mu] + f] = 2 * mu + 1
                    pick[self.slot[2 * mu + 1] + f, s] = 1
                    pick_link[self.ghost[mu] + f, s] = 1
                else:
                    code[s, s + strides[mu]] = 2 * mu + 1
                if at[mu] == 0:
                    code[s, self.sites + self.slot[2 * mu + 1] + f] = 2 * mu + 2
                    pick[self.slot[2 * mu] + f, s] = 1
                    below[mu * self.sites + s, self.sites + self.ghost[mu] + f] = 1
                else:
                    code[s, s - strides[mu]] = 2 * mu + 2
                    below[mu * self.sites + s, s - strides[mu]] = 1
        self.code, self.pick, self.pick_link, self.below = code, pick, pick_link, below


def dot(a, b):
    return jnp.dot(a, b, preferred_element_type=F32)


def main_kernel(plan, counts, scale, reduce_here, *refs):
    (v_ref, lt_ref, tab_ref, code_ref, pick_ref, pickl_ref, below_ref, smeared_ref, out_ref,
     v1, v2, pk1, pk2, lk, lg, mh, ml, acc, half_out, half_in, plane_out, plane_in, z_out, z_in,
     ssem, rsem) = refs
    sites, cols, parts = plan.sites, plan.cols, 6
    me = [lax.axis_index(a) for a in AXES]
    nx, ny, nz = counts

    def neighbour(mu, step):
        at = list(me)
        at[mu] = lax.rem(at[mu] + step + counts[mu], counts[mu])
        return tuple(at)

    ny2 = ny // 2
    nq = nx * ny2
    h = lax.rem(me[1], 2)
    q = me[0] * ny2 + me[1] // 2
    partner = (me[0], me[1] + 1 - 2 * h, me[2])

    def plane_at(index):
        return (index // ny2, lax.rem(index, ny2) * 2 + h, me[2])

    greeted = [neighbour(mu, step) for mu in range(3) for step in (-1, 1)]
    if reduce_here:
        greeted += [partner]
        greeted += [plane_at(lax.rem(q + r, nq)) for r in range(1, nq)]
        greeted += [(me[0], me[1], lax.rem(me[2] + r, nz)) for r in range(1, nz)]
    barrier = pltpu.get_barrier_semaphore()
    for device in greeted:
        pl.semaphore_signal(barrier, inc=1, device_id=device, device_id_type=MESH)

    used = [0]

    def copy(src, dst, device):
        k = used[0]
        used[0] += 1
        return pltpu.make_async_remote_copy(
            src_ref=src, dst_ref=dst, send_sem=ssem.at[k], recv_sem=rsem.at[k],
            device_id=device, device_id_type=MESH)

    pick = pick_ref[...]

    def fill(buf, packed, part, value):
        buf[part, 0:sites, :] = value
        packed[part] = dot(pick, value).astype(BF16)

    rest = sites + plan.halo
    for buf in (v1, v2):
        if rest < cols:
            buf[:, rest:cols, :] = jnp.zeros((parts, cols - rest, buf.shape[2]), BF16)
    lt = lt_ref[...]
    lk[...] = dot(pickl_ref[...], lt).astype(BF16)
    lg[0:sites, :] = lt
    used_rows = sites + plan.ghosts
    if used_rows < plan.link_rows:
        lg[used_rows:, :] = jnp.zeros((plan.link_rows - used_rows, lg.shape[1]), BF16)
    for part in range(parts):
        fill(v1, pk1, part, v_ref[part])
    pl.semaphore_wait(barrier, len(greeted))

    sends = []
    links = []
    for mu in range(3):
        g, n = plan.ghost[mu], plan.face[mu]
        links.append(copy(lk.at[g:g + n, :], lg.at[sites + g:sites + g + n, :], neighbour(mu, 1)))
        links[-1].start()

    def exchange(packed, buf):
        made = []
        for mu in (2, 0, 1):
            for side in range(2):
                o, n = plan.slot[2 * mu + side], plan.face[mu]
                made.append(copy(packed.at[:, o:o + n, :],
                                 buf.at[:, sites + o:sites + o + n, :],
                                 neighbour(mu, 2 * side - 1)))
                made[-1].start()
        return made

    halo1 = exchange(pk1, v1)
    for c in links:
        c.wait_recv()
    sends += links
    down = dot(below_ref[...], lg[...])
    here = lt.astype(F32)
    masks = [code_ref[...] == d + 1 for d in range(6)]
    shape = (sites, cols)
    for part, store in ((0, mh), (1, ml)):
        for i in range(3):
            for j in range(3):
                for c in range(2):
                    total = jnp.zeros(shape, F32)
                    for mu in range(3):
                        k = part * 128 + ((mu * 2 + c) * 3 + i) * 3 + j
                        value = here[:, k:k + 1]
                        total = jnp.where(masks[2 * mu], jnp.broadcast_to(value, shape), total)
                        k = part * 128 + ((mu * 2 + c) * 3 + j) * 3 + i
                        value = down[mu * sites:(mu + 1) * sites, k:k + 1]
                        if c:
                            value = -value
                        total = jnp.where(masks[2 * mu + 1], jnp.broadcast_to(value, shape), total)
                    total = total.astype(BF16)

                    def put(ro, co, val):
                        r0, c0 = (ro * 3 + i) * sites, (co * 3 + j) * cols
                        store[r0:r0 + sites, c0:c0 + cols] = val

                    if c == 0:
                        put(0, 0, total)
                        put(1, 1, total)
                    else:
                        put(1, 0, total)
                        put(0, 1, -total)

    def hop(buf):
        field = buf[...].reshape(parts * cols, buf.shape[2])
        return dot(mh[...], field) + dot(ml[...], field)

    for c in halo1:
        c.wait_recv()
    sends += halo1
    first = (hop(v1) / 6.0).astype(BF16)
    for part in range(parts):
        fill(v2, pk2, part, first[part * sites:(part + 1) * sites])
    halo2 = exchange(pk2, v2)
    for c in halo2:
        c.wait_recv()
    sends += halo2
    vectors = v_ref[...].reshape(parts * sites, v_ref.shape[2]).astype(F32)
    smeared = (2.0 * hop(v2) / 6.0 - vectors).astype(BF16)
    smeared_ref[...] = smeared.reshape(smeared_ref.shape)
    wide = smeared.astype(F32)
    rows = 3 * sites
    real_w, imag_w = wide[:rows], wide[rows:]
    left = jnp.transpose(wide).astype(BF16)
    moms = out_ref.shape[0] // 2
    width = v_ref.shape[2]
    for m in range(moms):
        cos_b = jnp.concatenate([tab_ref[:, 2 * m:2 * m + 1]] * 3, axis=0)
        sin_b = jnp.concatenate([tab_ref[:, 2 * m + 1:2 * m + 2]] * 3, axis=0)
        real_z = (cos_b * real_w + sin_b * imag_w).astype(BF16)
        imag_z = (cos_b * imag_w - sin_b * real_w).astype(BF16)
        acc[m] = dot(left, jnp.concatenate([real_z, imag_z], axis=0)) * scale
        acc[moms + m] = dot(left, jnp.concatenate([imag_z, -real_z], axis=0)) * scale

    if not reduce_here:
        out_ref[...] = acc[...]
        for c in sends:
            c.wait_send()
        return

    chunks = 2 * moms
    half = width // 2
    keep = pl.multiple_of(h * half, half)
    give = pl.multiple_of((1 - h) * half, half)
    half_out[...] = acc[:, pl.ds(give, half), :].astype(BF16)
    c = copy(half_out, half_in, partner)
    c.start()
    c.wait_recv()
    sends.append(c)
    piece = half // nq
    total = acc[:, pl.ds(keep, half), :] + half_in[...].astype(F32)
    acc[:, pl.ds(keep, half), :] = total
    plane_out[...] = total.astype(BF16)
    stage = []
    for r in range(1, nq):
        p = lax.rem(q + r, nq)
        c = copy(plane_out.at[:, pl.ds(pl.multiple_of(p * piece, piece), piece), :],
                 plane_in.at[r - 1], plane_at(p))
        c.start()
        stage.append(c)
    mine = pl.multiple_of(h * half + q * piece, piece)
    total = acc[:, pl.ds(mine, piece), :]
    for r in range(1, nq):
        stage[r - 1].wait_recv()
        total = total + plane_in[r - 1].astype(F32)
    sends += stage
    acc[:, pl.ds(mine, piece), :] = total
    z_out[...] = total.astype(BF16)
    per = chunks // nz
    stage = []
    for r in range(1, nz):
        p = lax.rem(me[2] + r, nz)
        c = copy(z_out.at[pl.ds(p * per, per)], z_in.at[r - 1], (me[0], me[1], p))
        c.start()
        stage.append(c)
    total = acc[pl.ds(me[2] * per, per), pl.ds(mine, piece), :]
    for r in range(1, nz):
        stage[r - 1].wait_recv()
        total = total + z_in[r - 1].astype(F32)
    sends += stage
    out_ref[pl.ds(me[2] * per, per), pl.ds(mine, piece), :] = total.astype(BF16)

    def gather(pairs):
        made = []
        for block, device, _ in pairs:
            made.append(copy(block, block, device))
            made[-1].start()
        for (_, device, back), c, k in zip(pairs, made, range(used[0] - len(made), used[0])):
            pltpu.make_async_remote_copy(
                src_ref=back, dst_ref=back, send_sem=ssem.at[k], recv_sem=rsem.at[k],
                device_id=device, device_id_type=MESH).wait_recv()
        sends.extend(made)

    def z_block(z):
        return out_ref.at[pl.ds(z * per, per), pl.ds(mine, piece), :]

    gather([(z_block(me[2]), (me[0], me[1], lax.rem(me[2] + r, nz)),
             z_block(lax.rem(me[2] + nz - r, nz))) for r in range(1, nz)])

    def plane_block(p):
        return out_ref.at[:, pl.ds(pl.multiple_of(h * half + p * piece, piece), piece), :]

    gather([(plane_block(q), plane_at(lax.rem(q + r, nq)), plane_block(lax.rem(q + nq - r, nq)))
            for r in range(1, nq)])
    gather([(out_ref.at[:, pl.ds(keep, half), :], partner, out_ref.at[:, pl.ds(give, half), :])])
    for c in sends:
        c.wait_send()


def smear_and_project(plan, counts, scale, fields, links, tables, moms):
    parts, sites, width = fields.shape
    chunks = 2 * moms
    nx, ny, nz = counts
    nq = max(nx * (ny // 2), 1)
    half = width // 2
    reduce_here = ny % 2 == 0 and half % (16 * nq) == 0 and chunks % nz == 0 and nz > 1 and nq > 1
    vm = pltpu.VMEM
    if reduce_here:
        extra = [
            vm((chunks, half, width), BF16), vm((chunks, half, width), BF16),
            vm((chunks, half, width), BF16), vm((nq - 1, chunks, half // nq, width), BF16),
            vm((chunks, half // nq, width), BF16),
            vm((nz - 1, chunks // nz, half // nq, width), BF16),
        ]
        copies = 3 + 12 + 2 * (1 + (nq - 1) + (nz - 1))
    else:
        extra = [vm((8, 128), BF16)] * 6
        copies = 3 + 12
    vmem = pl.BlockSpec(memory_space=pltpu.VMEM)
    return pl.pallas_call(
        functools.partial(main_kernel, plan, counts, scale, reduce_here),
        out_shape=(
            jax.ShapeDtypeStruct((parts, sites, width), BF16),
            jax.ShapeDtypeStruct((chunks, width, width), BF16 if reduce_here else F32),
        ),
        in_specs=[vmem] * 7,
        out_specs=(vmem, vmem),
        scratch_shapes=[
            vm((parts, plan.cols, width), BF16), vm((parts, plan.cols, width), BF16),
            vm((parts, plan.halo, width), BF16), vm((parts, plan.halo, width), BF16),
            vm((plan.ghosts, 256), BF16), vm((plan.link_rows, 256), BF16),
            vm((parts * sites, parts * plan.cols), BF16),
            vm((parts * sites, parts * plan.cols), BF16),
            vm((chunks, width, width), F32),
            *extra,
            pltpu.SemaphoreType.DMA((copies,)), pltpu.SemaphoreType.DMA((copies,)),
        ],
        compiler_params=pltpu.CompilerParams(
            collective_id=0, has_side_effects=True, vmem_limit_bytes=48 << 20),
        name="smear_project",
    )(fields, links, tables, jnp.asarray(plan.code), jnp.asarray(plan.pick, BF16),
      jnp.asarray(plan.pick_link, BF16), jnp.asarray(plan.below, BF16)), reduce_here


def sandwich_kernel(moms, spins, cols, ft_ref, p_ref, out_ref, pt, rhs, inner):
    width = p_ref.shape[1]
    for c in range(2):
        for s in range(spins):
            block = p_ref[c, :, s * cols:(s + 1) * cols]
            pt[s * cols:(s + 1) * cols, c * width:(c + 1) * width] = jnp.transpose(block)
    for s in range(spins):
        real_p = p_ref[0, :, s * cols:(s + 1) * cols]
        imag_p = p_ref[1, :, s * cols:(s + 1) * cols]
        r0 = s * 2 * width
        rhs[r0:r0 + width, 0:cols] = real_p
        rhs[r0:r0 + width, cols:2 * cols] = imag_p
        rhs[r0 + width:r0 + 2 * width, 0:cols] = -imag_p
        rhs[r0 + width:r0 + 2 * width, cols:2 * cols] = real_p
    left = pt[...]
    for m in range(moms):
        real_f = ft_ref[m]
        imag_f = ft_ref[moms + m]
        pair = (jnp.concatenate([real_f, imag_f], axis=0), jnp.concatenate([imag_f, -real_f], axis=0))
        for c in range(2):
            value = dot(left, pair[c]).astype(BF16)
            for s in range(spins):
                at = (s * 2 + c) * width
                inner[:, at:at + width] = value[s * cols:(s + 1) * cols]
        both = dot(inner[...], rhs[...]).astype(BF16)
        out_ref[m, 0] = both[:, :cols]
        out_ref[m, 1] = both[:, cols:]


def sandwich_of(ft, peram, spins, cols):
    chunks, width, _ = ft.shape
    moms = chunks // 2
    vmem = pl.BlockSpec(memory_space=pltpu.VMEM)
    return pl.pallas_call(
        functools.partial(sandwich_kernel, moms, spins, cols),
        out_shape=jax.ShapeDtypeStruct((moms, 2, cols, cols), BF16),
        in_specs=[vmem, vmem],
        out_specs=vmem,
        scratch_shapes=[
            pltpu.VMEM((spins * cols, 2 * width), BF16),
            pltpu.VMEM((spins * 2 * width, 2 * cols), BF16),
            pltpu.VMEM((cols, spins * 2 * width), BF16),
        ],
        compiler_params=pltpu.CompilerParams(vmem_limit_bytes=32 << 20),
        name="sandwich",
    )(ft, peram)


def per_device(counts, vectors, gauge_links, momenta, perambulator):
    dims = vectors.shape[2:5]
    width = vectors.shape[5]
    moms = momenta.shape[0]
    plan = Plan(dims)
    sites = plan.sites
    cells = [dims[a] * counts[a] for a in range(3)]
    fields = vectors.reshape(6, sites, width)
    links = jnp.transpose(gauge_links.reshape(54, sites))
    links = jnp.pad(links, ((0, 0), (0, 128 - 54)))
    high = lax.reduce_precision(links, 8, 7)
    links = jnp.concatenate([high.astype(BF16), (links - high).astype(BF16)], axis=1)
    index = lax.broadcasted_iota(jnp.int32, (sites, 128), 0)
    lane = lax.broadcasted_iota(jnp.int32, (sites, 128), 1)
    spot = (index // (dims[1] * dims[2]), index // dims[2] % dims[1], index % dims[2])
    theta = jnp.zeros((sites, 128), F32)
    for a in range(3):
        at = lax.axis_index(AXES[a]) * dims[a] + spot[a]
        factor = jnp.zeros((sites, 128), jnp.int32)
        for m in range(moms):
            factor = jnp.where(lane // 2 == m, momenta[m, a], factor)
        theta = theta + (factor * at % cells[a]).astype(F32) / cells[a]
    theta = 2.0 * math.pi * theta
    tables = jnp.where(lane % 2 == 0, jnp.cos(theta), jnp.sin(theta))
    scale = 1.0 / math.sqrt(3.0 * cells[0] * cells[1] * cells[2])
    (smeared, ft), reduced = smear_and_project(plan, counts, scale, fields, links, tables, moms)
    if not reduced:
        ft = lax.psum(ft, AXES).astype(BF16)
    count, _, _, spins, cols = perambulator.shape
    rows = perambulator.reshape(count, 2, width, spins * cols)
    sandwich = jnp.stack([sandwich_of(ft, rows[n], spins, cols) for n in range(count)])
    return smeared.reshape(vectors.shape), sandwich


def solution(mesh):
    counts = tuple(mesh.shape[a] for a in AXES)
    return jax.shard_map(
        functools.partial(per_device, counts),
        mesh=mesh,
        in_specs=(
            P(None, None, "gx", "gy", "gz", None),
            P(None, None, None, None, "gx", "gy", "gz"),
            P(),
            P(("gx", "gy", "gz"), None, None, None, None),
        ),
        out_specs=(
            P(None, None, "gx", "gy", "gz", None),
            P(("gx", "gy", "gz"), None, None, None, None),
        ),
        check_vma=False,
    )
```

time: 125 us -> 51 us (0.41)
  blocking collectives: 50.9 us -> 0 us
  Pallas kernels: 0 us -> 40.3 us
  waiting for transfers between devices: 24.4 us -> 0 us
  starting transfers between devices: 20.1 us -> 0 us
  local copies, waits for them, and re-layouts: 13.1 us -> 5.55 us
  matrix products: 5.53 us -> 0 us
  other arithmetic: 9.53 us -> 4.06 us
    psum x1 -> x0, blocking collectives: 50.9 us -> none  [per_device(): gathered = lax.psum(elemental_rows, ('gx', 'gy', 'gz')).astype(jnp.bfloat16)]
    pallas_call x0 -> x2, Pallas kernels: none -> 40.3 us  [the longest x1 37.1 us: smear_and_project(): pl.pallas_call(functools.partial(main_kernel, plan, counts, scale, reduce...]
    ppermute x15 -> x0, waiting for transfers between devices: 24.4 us -> none  [the longest x6 12.5 us: padded_2(): lax.ppermute(tail, axis, [(i, (i + 1) % count) for i in range(count)])]
    ppermute x15 -> x0, starting transfers between devices: 20.1 us -> none  [the longest x6 10.9 us: padded_2(): lax.ppermute(head, axis, [((i + 1) % count, i) for i in range(count)])]
    dot_general x3 -> x0, matrix products: 5.53 us -> none  [the longest x1 2.86 us: per_device(): jnp.einsum('nmcrk,ndrl->nmcdkl', inner_rows, peram_parts, preferred_eleme...]
    another operation x6 -> x1, local copies, waits for them, and re-layouts: 5.6 us -> 0.75 us  [per_device(): rows[n]]
    add x16 -> x0, other arithmetic: 4.69 us -> none  [the longest x12 4.6 us: link_times(): real_part = add_real if real_part is None else real_part + add_real]
    select_n x0 -> x1, other arithmetic: none -> 4 us  [per_device(): tables = jnp.where(lane % 2 == 0, jnp.cos(theta), jnp.sin(theta))]
  transfers between devices with their start and end apart: 15 -> 0, of which waited for: 10 -> 0; matrix products, arithmetic and copies ran while one was open for 8% -> 0% of each run, Pallas kernels for 0% -> 0%
where the time goes in v1:
time: 51 us; the launch traced here: 50.7 us
  Pallas kernels  40.3 us (79%)
  local copies, waits for them, and re-layouts  5.55 us (11%)
  other arithmetic  4.06 us (8%)
  between operations  0.8 us (2%)
    pallas_call x1, Pallas kernels, smear_and_project(): pl.pallas_call(functools.partial(main_kernel, plan, counts, scale, reduce...  37.1 us
    select_n x1, other arithmetic, per_device(): tables = jnp.where(lane % 2 == 0, jnp.cos(theta), jnp.sin(theta))  4 us
    pallas_call x1, Pallas kernels, sandwich_of(): pl.pallas_call(functools.partial(sandwich_kernel, moms, spins, cols), out...  3.17 us
    slice x1, local copies, waits for them, and re-layouts, per_device(): factor = jnp.where(lane // 2 == m, momenta[m, a], factor)  1.53 us
    reshape x2, local copies, waits for them, and re-layouts, per_device(): links = jnp.transpose(gauge_links.reshape(54, sites))  1.5 us

profile of v1, /device:TPU:0, one launch (start us, length us, event | category | flops | bytes accessed | tf_op | source)
XLA Modules:
  0.0 50.7 jit_solution(3312107078252319810)
XLA Ops:
  0.6 0.0 copy-start.4
  0.7 1.5 %fusion.24 = (s32[1,1]{1,0:T(1,128)}, s32[1,1]{1,0:T(1,128)}, s32[1,1]{1,0:T(1,128)}, s32[1,1]{1,0:T(1,128)}, s32[1,1]{1,0:T(1,128)}, /*index=5*/s32[1,1]{1,0:T(1,128)}) fusion(s32[2,3]{1,0:T(2,128)} %param.10), kind=kLoop, calls=%fused_computation.63 | loop fusion | bytes 48 | tf_op jit(solution)/shard_map/slice | solution.py:399
  2.3 4.0 %sine_select_fusion.refs_2_ = f32[64,128]{1,0:T(8,128)S(1)} fusion(s32[64]{0:T(128)S(1)} %get-tuple-element.20, s32[64]{0:T(128)S(1)} %get-tuple-element.25, s32[]{:T(128)S(6)} %mul.28, s32[]{:T(128)} %bitcast.6, s32[]{:T(128)} %bitcast.5, s32[64]{0:T(128)S(1)} %get-tuple-element.19, s32[64]{0:T(128)S(1)} %get-tuple-element.21, s32[]{:T(128)S(6)} %mul.26, ...), kind=kLoop, calls=%fused_computation.43 | loop fusion | flops 606208 | bytes 36836 | tf_op jit(solution)/shard_map/jit(_where)/select_n | solution.py:402
  6.3 1.4 %reshape.14 = f32[54,64]{1,0:T(8,128)S(1)} reshape(f32[3,2,3,3,4,4,4]{6,5,4,3,2,1,0:T(4,128)} %param.9) | data formatting | bytes 27648 | tf_op jit(solution)/shard_map/reshape | solution.py:387
  7.7 0.1 copy.11
  7.8 0.0 copy-start
  7.8 0.0 copy-start.1
  7.8 0.0 copy-start.2
  7.8 0.0 copy-start.3
  7.9 1.0 %reshape.13.refs_0_ = bf16[6,64,256]{2,1,0:T(8,128)(2,1)S(1)} reshape(bf16[2,3,4,4,4,256]{5,4,3,2,1,0:T(4,128)(2,1)} %param.8) | data formatting | bytes 393216 | tf_op jit(solution)/shard_map/reshape | solution.py:386
  8.9 0.0 copy-done
  8.9 0.0 copy-done.1
  8.9 0.0 copy-done.2
  8.9 0.0 copy-done.3
  8.9 37.1 %smear_project.1 = (bf16[6,64,256]{2,1,0:T(8,128)(2,1)S(1)}, bf16[4,256,256]{2,1,0:T(8,128)(2,1)S(1)}) custom-call(bf16[6,64,256]{2,1,0:T(8,128)(2,1)S(1)} %reshape.13.refs_0_, bf16[64,256]{1,0:T(8,128)(2,1)S(1)} %pad_maximum_fusion.refs_1_, f32[64,128]{1,0:T(8,128)S(1)} %sine_select_fusion.refs_2_, s32[64,256]{1,0:T(8,128)S(1)} %copy-done, ...), custom_call_target="tpu_custom_call" | custom-call | tf_op jit(solution)/shard_map/smear_project/pallas_call | solution.py:306
  46.1 0.7 %reshape.15 = bf16[2,3,4,4,4,256]{5,4,3,2,1,0:T(4,128)(2,1)} reshape(bf16[6,64,256]{2,1,0:T(8,128)(2,1)S(1)} %get-tuple-element.4) | data formatting | bytes 393216 | tf_op jit(solution)/shard_map/reshape | solution.py:410
  46.8 0.0 copy-done.4
  46.8 0.7 %squeeze_reshape.3.p_ref = bf16[2,256,1024]{2,1,0:T(8,128)(2,1)S(1)} reshape(bf16[1,2,256,4,256]{4,3,2,1,0:T(4,128)(2,1)S(1)} %copy-done.4) | data formatting | bytes 2097152 | tf_op jit(solution)/shard_map/squeeze;reshape | solution.py:409
  47.5 3.2 %sandwich.1 = bf16[2,2,256,256]{3,2,1,0:T(8,128)(2,1)} custom-call(bf16[4,256,256]{2,1,0:T(8,128)(2,1)S(1)} %get-tuple-element.5.ft_ref, bf16[2,256,1024]{2,1,0:T(8,128)(2,1)S(1)} %squeeze_reshape.3.p_ref), custom_call_target="tpu_custom_call" | custom-call | tf_op jit(solution)/shard_map/sandwich/pallas_call | solution.py:364
  (10 shorter events, 0.1 us)
Async XLA Ops:
  0.6 46.2 %copy-start.4 = (bf16[1,2,256,4,256]{4,3,2,1,0:T(4,128)(2,1)S(1)}, bf16[1,2,256,4,256]{4,3,2,1,0:T(4,128)(2,1)}, u32[]{:S(2)}) copy-start(bf16[1,2,256,4,256]{4,3,2,1,0:T(4,128)(2,1)} %param.11) | copy-start | bytes 3145732
  7.8 1.1 %copy-start = (s32[64,256]{1,0:T(8,128)S(1)}, s32[64,256]{1,0:T(8,128)}, u32[]{:S(2)}) copy-start(s32[64,256]{1,0:T(8,128)} %constant.140.clone.refs_3_) | copy-start | bytes 196612
  7.8 1.1 %copy-start.1 = (bf16[192,112]{1,0:T(8,128)(2,1)S(1)}, bf16[192,112]{1,0:T(8,128)(2,1)}, u32[]{:S(2)}) copy-start(bf16[192,112]{1,0:T(8,128)(2,1)} %constant.143.clone.refs_6_) | copy-start | bytes 129028
  7.8 1.1 %copy-start.2 = (bf16[96,64]{1,0:T(8,128)(2,1)S(1)}, bf16[96,64]{1,0:T(8,128)(2,1)}, u32[]{:S(2)}) copy-start(bf16[96,64]{1,0:T(8,128)(2,1)} %constant.141.clone.refs_4_) | copy-start | bytes 36868
  7.8 1.1 %copy-start.3 = (bf16[48,64]{1,0:T(8,128)(2,1)S(1)}, bf16[48,64]{1,0:T(8,128)(2,1)}, u32[]{:S(2)}) copy-start(bf16[48,64]{1,0:T(8,128)(2,1)} %constant.142.clone.refs_5_) | copy-start | bytes 18436

commit v2 on v1

--- a/solution.py
+++ b/solution.py
@@ -64,9 +64,47 @@
     return jnp.dot(a, b, preferred_element_type=F32)
 
 
+def phase_table(plan, counts, me, mom_ref, moms):
+    dims = plan.dims
+    shape = (plan.sites, 128)
+    site = lax.broadcasted_iota(jnp.int32, shape, 0).astype(F32)
+    lane = lax.broadcasted_iota(jnp.int32, shape, 1)
+    yz, zz = dims[1] * dims[2], dims[2]
+    x = jnp.floor((site + 0.5) / yz)
+    rest = site - x * yz
+    y = jnp.floor((rest + 0.5) / zz)
+    spot = (x, y, rest - y * zz)
+    total = jnp.zeros(shape, F32)
+    for a in range(3):
+        at = spot[a] + (me[a] * dims[a]).astype(F32)
+        cells = float(dims[a] * counts[a])
+        factor = jnp.zeros(shape, F32)
+        for m in range(moms):
+            factor = jnp.where(lane >= 2 * m, mom_ref[m, a].astype(F32), factor)
+        product = factor * at
+        total = total + (product - jnp.floor(product / cells) * cells) / cells
+    theta = 2.0 * math.pi * total
+    return jnp.where(lane % 2 == 0, jnp.cos(theta), jnp.sin(theta))
+
+
+def prepare(p_ref, pt_ref, rhs_ref, width):
+    cols = rhs_ref.shape[1] // 2
+    spins = pt_ref.shape[0] // cols
+    for s in range(spins):
+        real_p = p_ref[0, :, s * cols:(s + 1) * cols]
+        imag_p = p_ref[1, :, s * cols:(s + 1) * cols]
+        pt_ref[s * cols:(s + 1) * cols, 0:width] = jnp.transpose(real_p)
+        pt_ref[s * cols:(s + 1) * cols, width:2 * width] = jnp.transpose(imag_p)
+        r0 = s * 2 * width
+        rhs_ref[r0:r0 + width, 0:cols] = real_p
+        rhs_ref[r0:r0 + width, cols:2 * cols] = imag_p
+        rhs_ref[r0 + width:r0 + 2 * width, 0:cols] = -imag_p
+        rhs_ref[r0 + width:r0 + 2 * width, cols:2 * cols] = real_p
+
+
 def main_kernel(plan, counts, scale, reduce_here, *refs):
-    (v_ref, lt_ref, tab_ref, code_ref, pick_ref, pickl_ref, below_ref, smeared_ref, out_ref,
-     v1, v2, pk1, pk2, lk, lg, mh, ml, acc, half_out, half_in, plane_out, plane_in, z_out, z_in,
+    (v_ref, lt_ref, mom_ref, code_ref, pick_ref, pickl_ref, below_ref, p_ref,
+     smeared_ref, out_ref, pt_ref, rhs_ref, tab, v1, v2, pk1, pk2, lk, lg, mh, ml, acc, half_out, half_in, plane_out, plane_in, z_out, z_in,
      ssem, rsem) = refs
     sites, cols, parts = plan.sites, plan.cols, 6
     me = [lax.axis_index(a) for a in AXES]
@@ -143,6 +181,7 @@
         return made
 
     halo1 = exchange(pk1, v1)
+    tab[...] = phase_table(plan, counts, me, mom_ref, out_ref.shape[0] // 2)
     for c in links:
         c.wait_recv()
     sends += links
@@ -201,89 +240,130 @@
     moms = out_ref.shape[0] // 2
     width = v_ref.shape[2]
     for m in range(moms):
-        cos_b = jnp.concatenate([tab_ref[:, 2 * m:2 * m + 1]] * 3, axis=0)
-        sin_b = jnp.concatenate([tab_ref[:, 2 * m + 1:2 * m + 2]] * 3, axis=0)
+        cos_b = jnp.concatenate([tab[:, 2 * m:2 * m + 1]] * 3, axis=0)
+        sin_b = jnp.concatenate([tab[:, 2 * m + 1:2 * m + 2]] * 3, axis=0)
         real_z = (cos_b * real_w + sin_b * imag_w).astype(BF16)
         imag_z = (cos_b * imag_w - sin_b * real_w).astype(BF16)
         acc[m] = dot(left, jnp.concatenate([real_z, imag_z], axis=0)) * scale
         acc[moms + m] = dot(left, jnp.concatenate([imag_z, -real_z], axis=0)) * scale
 
     if not reduce_here:
+        prepare(p_ref, pt_ref, rhs_ref, width)
         out_ref[...] = acc[...]
         for c in sends:
             c.wait_send()
         return
 
     chunks = 2 * moms
+    per = chunks // nz
     half = width // 2
+    piece = half // nq
     keep = pl.multiple_of(h * half, half)
     give = pl.multiple_of((1 - h) * half, half)
+    mine = pl.multiple_of(h * half + q * piece, piece)
+    z = me[2]
+
+    def plane_rows(p):
+        return pl.ds(pl.multiple_of(h * half + p * piece, piece), piece)
+
+    order = []
+    for k in range(nz - 1):
+        low = jnp.where(nz - 1 - k > z, nz - 1 - k, nz - 2 - k)
+        high = jnp.where(k < z, k, k + 1)
+        order.append(jnp.where(z < nz // 2, low, high))
+    order.append(z)
+    group = [pl.ds(p * per, per) for p in order]
+
     half_out[...] = acc[:, pl.ds(give, half), :].astype(BF16)
-    c = copy(half_out, half_in, partner)
-    c.start()
-    c.wait_recv()
-    sends.append(c)
-    piece = half // nq
-    total = acc[:, pl.ds(keep, half), :] + half_in[...].astype(F32)
-    acc[:, pl.ds(keep, half), :] = total
-    plane_out[...] = total.astype(BF16)
-    stage = []
-    for r in range(1, nq):
-        p = lax.rem(q + r, nq)
-        c = copy(plane_out.at[:, pl.ds(pl.multiple_of(p * piece, piece), piece), :],
-                 plane_in.at[r - 1], plane_at(p))
+    pair = []
+    for k in range(nz):
+        pair.append(copy(half_out.at[group[k]], half_in.at[group[k]], partner))
+        pair[-1].start()
+    plane = []
+    for k in range(nz):
+        pair[k].wait_recv()
+        total = acc[group[k], pl.ds(keep, half), :] + half_in[group[k]].astype(F32)
+        acc[group[k], pl.ds(keep, half), :] = total
+        plane_out[group[k]] = total.astype(BF16)
+        row = []
+        for r in range(1, nq):
+            p = lax.rem(q + r, nq)
+            row.append(copy(
+                plane_out.at[group[k], pl.ds(pl.multiple_of(p * piece, piece), piece), :],
+                plane_in.at[r - 1, group[k]], plane_at(p)))
+            row[-1].start()
+        plane.append(row)
+    prepare(p_ref, pt_ref, rhs_ref, width)
+    sends += pair
+    base = used[0]
+    for k in range(nz):
+        total = acc[group[k], pl.ds(mine, piece), :]
+        for r in range(1, nq):
+            plane[k][r - 1].wait_recv()
+            total = total + plane_in[r - 1, group[k]].astype(F32)
+        sends += plane[k]
+        if k < nz - 1:
+            z_out[k] = total.astype(BF16)
+            r = lax.rem(order[k] - z + nz, nz)
+            c = pltpu.make_async_remote_copy(
+                src_ref=z_out.at[k], dst_ref=z_in.at[r - 1], send_sem=ssem.at[base + k],
+                recv_sem=rsem.at[base + r - 1], device_id=(me[0], me[1], order[k]),
+                device_id_type=MESH)
+            c.start()
+            sends.append(c)
+    used[0] += nz - 1
+    for r in range(1, nz):
+        pltpu.make_async_remote_copy(
+            src_ref=z_out.at[r - 1], dst_ref=z_in.at[r - 1], send_sem=ssem.at[base + r - 1],
+            recv_sem=rsem.at[base + r - 1], device_id=partner,
+            device_id_type=MESH).wait_recv()
+        total = total + z_in[r - 1].astype(F32)
+    out_ref[group[nz - 1], pl.ds(mine, piece), :] = total.astype(BF16)
+
+    def block(k, rows):
+        return out_ref.at[group[k], rows, :]
+
+    def arrival(ref, index):
+        pltpu.make_async_remote_copy(
+            src_ref=ref, dst_ref=ref, send_sem=ssem.at[index], recv_sem=rsem.at[index],
+            device_id=partner, device_id_type=MESH).wait_recv()
+
+    base = used[0]
+    used[0] += nz - 1
+    own = block(nz - 1, plane_rows(q))
+    for k in range(nz - 1):
+        r = lax.rem(order[k] - z + nz, nz)
+        c = pltpu.make_async_remote_copy(
+            src_ref=own, dst_ref=own, send_sem=ssem.at[base + k],
+            recv_sem=rsem.at[base + r - 1], device_id=(me[0], me[1], order[k]),
+            device_id_type=MESH)
         c.start()
-        stage.append(c)
-    mine = pl.multiple_of(h * half + q * piece, piece)
-    total = acc[:, pl.ds(mine, piece), :]
-    for r in range(1, nq):
-        stage[r - 1].wait_recv()
-        total = total + plane_in[r - 1].astype(F32)
-    sends += stage
-    acc[:, pl.ds(mine, piece), :] = total
-    z_out[...] = total.astype(BF16)
-    per = chunks // nz
-    stage = []
-    for r in range(1, nz):
-        p = lax.rem(me[2] + r, nz)
-        c = copy(z_out.at[pl.ds(p * per, per)], z_in.at[r - 1], (me[0], me[1], p))
+        sends.append(c)
+    spread = {}
+    for k in reversed(range(nz)):
+        if k < nz - 1:
+            arrival(block(k, plane_rows(q)), base + lax.rem(z - order[k] + nz, nz) - 1)
+        spread[k] = used[0]
+        for r in range(1, nq):
+            c = copy(block(k, plane_rows(q)), block(k, plane_rows(q)), plane_at(lax.rem(q + r, nq)))
+            c.start()
+            sends.append(c)
+    pair = {}
+    for k in reversed(range(nz)):
+        for r in range(1, nq):
+            arrival(block(k, plane_rows(lax.rem(q + nq - r, nq))), spread[k] + r - 1)
+        pair[k] = used[0]
+        c = copy(block(k, pl.ds(keep, half)), block(k, pl.ds(keep, half)), partner)
         c.start()
-        stage.append(c)
-    total = acc[pl.ds(me[2] * per, per), pl.ds(mine, piece), :]
-    for r in range(1, nz):
-        stage[r - 1].wait_recv()
-        total = total + z_in[r - 1].astype(F32)
-    sends += stage
-    out_ref[pl.ds(me[2] * per, per), pl.ds(mine, piece), :] = total.astype(BF16)
-
-    def gather(pairs):
-        made = []
-        for block, device, _ in pairs:
-            made.append(copy(block, block, device))
-            made[-1].start()
-        for (_, device, back), c, k in zip(pairs, made, range(used[0] - len(made), used[0])):
-            pltpu.make_async_remote_copy(
-                src_ref=back, dst_ref=back, send_sem=ssem.at[k], recv_sem=rsem.at[k],
-                device_id=device, device_id_type=MESH).wait_recv()
-        sends.extend(made)
-
-    def z_block(z):
-        return out_ref.at[pl.ds(z * per, per), pl.ds(mine, piece), :]
-
-    gather([(z_block(me[2]), (me[0], me[1], lax.rem(me[2] + r, nz)),
-             z_block(lax.rem(me[2] + nz - r, nz))) for r in range(1, nz)])
-
-    def plane_block(p):
-        return out_ref.at[:, pl.ds(pl.multiple_of(h * half + p * piece, piece), piece), :]
-
-    gather([(plane_block(q), plane_at(lax.rem(q + r, nq)), plane_block(lax.rem(q + nq - r, nq)))
-            for r in range(1, nq)])
-    gather([(out_ref.at[:, pl.ds(keep, half), :], partner, out_ref.at[:, pl.ds(give, half), :])])
+        sends.append(c)
+    for k in reversed(range(nz)):
+        arrival(block(k, pl.ds(give, half)), pair[k])
     for c in sends:
         c.wait_send()
 
 
-def smear_and_project(plan, counts, scale, fields, links, tables, moms):
+def smear_and_project(plan, counts, scale, fields, links, momenta, rows, cols):
+    moms = momenta.shape[0]
     parts, sites, width = fields.shape
     chunks = 2 * moms
     nx, ny, nz = counts
@@ -295,10 +375,10 @@
         extra = [
             vm((chunks, half, width), BF16), vm((chunks, half, width), BF16),
             vm((chunks, half, width), BF16), vm((nq - 1, chunks, half // nq, width), BF16),
-            vm((chunks, half // nq, width), BF16),
+            vm((nz - 1, chunks // nz, half // nq, width), BF16),
             vm((nz - 1, chunks // nz, half // nq, width), BF16),
         ]
-        copies = 3 + 12 + 2 * (1 + (nq - 1) + (nz - 1))
+        copies = 3 + 12 + 2 * (nz + nz * (nq - 1) + (nz - 1))
     else:
         extra = [vm((8, 128), BF16)] * 6
         copies = 3 + 12
@@ -308,10 +388,13 @@
         out_shape=(
             jax.ShapeDtypeStruct((parts, sites, width), BF16),
             jax.ShapeDtypeStruct((chunks, width, width), BF16 if reduce_here else F32),
+            jax.ShapeDtypeStruct((rows.shape[2], 2 * width), BF16),
+            jax.ShapeDtypeStruct((rows.shape[2] // cols * 2 * width, 2 * cols), BF16),
         ),
-        in_specs=[vmem] * 7,
-        out_specs=(vmem, vmem),
+        in_specs=[vmem, vmem, pl.BlockSpec(memory_space=pltpu.SMEM)] + [vmem] * 5,
+        out_specs=(vmem,) * 4,
         scratch_shapes=[
+            vm((sites, 128), F32),
             vm((parts, plan.cols, width), BF16), vm((parts, plan.cols, width), BF16),
             vm((parts, plan.halo, width), BF16), vm((parts, plan.halo, width), BF16),
             vm((plan.ghosts, 256), BF16), vm((plan.link_rows, 256), BF16),
@@ -324,24 +407,12 @@
         compiler_params=pltpu.CompilerParams(
             collective_id=0, has_side_effects=True, vmem_limit_bytes=48 << 20),
         name="smear_project",
-    )(fields, links, tables, jnp.asarray(plan.code), jnp.asarray(plan.pick, BF16),
-      jnp.asarray(plan.pick_link, BF16), jnp.asarray(plan.below, BF16)), reduce_here
-
-
-def sandwich_kernel(moms, spins, cols, ft_ref, p_ref, out_ref, pt, rhs, inner):
-    width = p_ref.shape[1]
-    for c in range(2):
-        for s in range(spins):
-            block = p_ref[c, :, s * cols:(s + 1) * cols]
-            pt[s * cols:(s + 1) * cols, c * width:(c + 1) * width] = jnp.transpose(block)
-    for s in range(spins):
-        real_p = p_ref[0, :, s * cols:(s + 1) * cols]
-        imag_p = p_ref[1, :, s * cols:(s + 1) * cols]
-        r0 = s * 2 * width
-        rhs[r0:r0 + width, 0:cols] = real_p
-        rhs[r0:r0 + width, cols:2 * cols] = imag_p
-        rhs[r0 + width:r0 + 2 * width, 0:cols] = -imag_p
-        rhs[r0 + width:r0 + 2 * width, cols:2 * cols] = real_p
+    )(fields, links, momenta, jnp.asarray(plan.code), jnp.asarray(plan.pick, BF16),
+      jnp.asarray(plan.pick_link, BF16), jnp.asarray(plan.below, BF16), rows), reduce_here
+
+
+def sandwich_kernel(moms, spins, cols, ft_ref, pt, rhs, out_ref, inner):
+    width = ft_ref.shape[1]
     left = pt[...]
     for m in range(moms):
         real_f = ft_ref[m]
@@ -357,29 +428,46 @@
         out_ref[m, 1] = both[:, cols:]
 
 
-def sandwich_of(ft, peram, spins, cols):
+def sandwich_of(ft, pt, rhs, spins, cols):
     chunks, width, _ = ft.shape
     moms = chunks // 2
     vmem = pl.BlockSpec(memory_space=pltpu.VMEM)
     return pl.pallas_call(
         functools.partial(sandwich_kernel, moms, spins, cols),
         out_shape=jax.ShapeDtypeStruct((moms, 2, cols, cols), BF16),
-        in_specs=[vmem, vmem],
+        in_specs=[vmem] * 3,
         out_specs=vmem,
         scratch_shapes=[
-            pltpu.VMEM((spins * cols, 2 * width), BF16),
-            pltpu.VMEM((spins * 2 * width, 2 * cols), BF16),
             pltpu.VMEM((cols, spins * 2 * width), BF16),
         ],
         compiler_params=pltpu.CompilerParams(vmem_limit_bytes=32 << 20),
         name="sandwich",
-    )(ft, peram)
+    )(ft, pt, rhs)
+
+
+def prepare_one(rows, cols):
+    width = rows.shape[1]
+    spins = rows.shape[2] // cols
+    vmem = pl.BlockSpec(memory_space=pltpu.VMEM)
+
+    def kernel(p_ref, pt_ref, rhs_ref):
+        prepare(p_ref, pt_ref, rhs_ref, width)
+
+    return pl.pallas_call(
+        kernel,
+        out_shape=(
+            jax.ShapeDtypeStruct((spins * cols, 2 * width), BF16),
+            jax.ShapeDtypeStruct((spins * 2 * width, 2 * cols), BF16),
+        ),
+        in_specs=[vmem],
+        out_specs=(vmem, vmem),
+        name="prepare",
+    )(rows)
 
 
 def per_device(counts, vectors, gauge_links, momenta, perambulator):
     dims = vectors.shape[2:5]
     width = vectors.shape[5]
-    moms = momenta.shape[0]
     plan = Plan(dims)
     sites = plan.sites
     cells = [dims[a] * counts[a] for a in range(3)]
@@ -388,25 +476,18 @@
     links = jnp.pad(links, ((0, 0), (0, 128 - 54)))
     high = lax.reduce_precision(links, 8, 7)
     links = jnp.concatenate([high.astype(BF16), (links - high).astype(BF16)], axis=1)
-    index = lax.broadcasted_iota(jnp.int32, (sites, 128), 0)
-    lane = lax.broadcasted_iota(jnp.int32, (sites, 128), 1)
-    spot = (index // (dims[1] * dims[2]), index // dims[2] % dims[1], index % dims[2])
-    theta = jnp.zeros((sites, 128), F32)
-    for a in range(3):
-        at = lax.axis_index(AXES[a]) * dims[a] + spot[a]
-        factor = jnp.zeros((sites, 128), jnp.int32)
-        for m in range(moms):
-            factor = jnp.where(lane // 2 == m, momenta[m, a], factor)
-        theta = theta + (factor * at % cells[a]).astype(F32) / cells[a]
-    theta = 2.0 * math.pi * theta
-    tables = jnp.where(lane % 2 == 0, jnp.cos(theta), jnp.sin(theta))
     scale = 1.0 / math.sqrt(3.0 * cells[0] * cells[1] * cells[2])
-    (smeared, ft), reduced = smear_and_project(plan, counts, scale, fields, links, tables, moms)
+    count, _, _, spins, cols = perambulator.shape
+    rows = perambulator.reshape(count, 2, width, spins * cols)
+    (smeared, ft, pt, rhs), reduced = smear_and_project(
+        plan, counts, scale, fields, links, momenta, rows[0], cols)
     if not reduced:
         ft = lax.psum(ft, AXES).astype(BF16)
-    count, _, _, spins, cols = perambulator.shape
-    rows = perambulator.reshape(count, 2, width, spins * cols)
-    sandwich = jnp.stack([sandwich_of(ft, rows[n], spins, cols) for n in range(count)])
+    sandwich = [sandwich_of(ft, pt, rhs, spins, cols)]
+    for n in range(1, count):
+        pt, rhs = prepare_one(rows[n], cols)
+        sandwich.append(sandwich_of(ft, pt, rhs, spins, cols))
+    sandwich = jnp.stack(sandwich)
     return smeared.reshape(vectors.shape), sandwich
 
 

time: 51 us -> 52.5 us (1.029)
  local copies, waits for them, and re-layouts: 5.55 us -> 12.2 us
  other arithmetic: 4.06 us -> 0.63 us
  Pallas kernels: 40.3 us -> 38.5 us
    unnamed x10 -> x20, local copies, waits for them, and re-layouts: 0.03 us -> 7.16 us
    select_n x1 -> x0, other arithmetic: 4 us -> none  [per_device(): tables = jnp.where(lane % 2 == 0, jnp.cos(theta), jnp.sin(theta))]
    pallas_call x1, Pallas kernels: 37.1 us -> 35.4 us  [smear_and_project(): pl.pallas_call(functools.partial(main_kernel, plan, counts, scale, reduce...]
    slice x1 -> x0, local copies, waits for them, and re-layouts: 1.53 us -> none  [per_device(): factor = jnp.where(lane // 2 == m, momenta[m, a], factor)]
    another operation x1, local copies, waits for them, and re-layouts: 0.75 us -> 1.79 us  [per_device(): rows[0]]
    concatenate x1, other arithmetic: 0.01 us -> 0.62 us  [per_device(): jnp.concatenate([high.astype(BF16), (links - high).astype(BF16)], axis=1)]
where the time goes in v2:
time: 52.5 us; the launch traced here: 52 us
  Pallas kernels  38.5 us (73%)
  local copies, waits for them, and re-layouts  12.2 us (23%)
  between operations  0.71 us (1%)
  other arithmetic  0.63 us (1%)
    pallas_call x1, Pallas kernels, smear_and_project(): pl.pallas_call(functools.partial(main_kernel, plan, counts, scale, reduce...  35.4 us
    unnamed x20, local copies, waits for them, and re-layouts  7.16 us
    pallas_call x1, Pallas kernels, sandwich_of(): pl.pallas_call(functools.partial(sandwich_kernel, moms, spins, cols), out...  3.13 us
    another operation x1, local copies, waits for them, and re-layouts, per_device(): rows[0]  1.79 us
    reshape x2, local copies, waits for them, and re-layouts, per_device(): links = jnp.transpose(gauge_links.reshape(54, sites))  1.51 us

profile of v2, /device:TPU:0, one launch (start us, length us, event | category | flops | bytes accessed | tf_op | source)
XLA Modules:
  0.0 52.0 jit_solution(2142448674937370153)
XLA Ops:
  0.6 0.0 copy-start.8
  0.6 0.0 copy-start.9
  0.7 1.4 %reshape.14 = f32[54,64]{1,0:T(8,128)S(1)} reshape(f32[3,2,3,3,4,4,4]{6,5,4,3,2,1,0:T(4,128)} %param.9) | data formatting | bytes 27648 | tf_op jit(solution)/shard_map/reshape | solution.py:475
  2.1 0.1 copy.11
  2.2 0.6 %pad_maximum_fusion.refs_1_ = bf16[64,256]{1,0:T(8,128)(2,1)} fusion(bf16[64,128]{1,0:T(8,128)(2,1)S(1)} %get-tuple-element.11, bf16[64,128]{1,0:T(8,128)(2,1)S(1)} %get-tuple-element.10), kind=kLoop, calls=%fused_computation.3 | loop fusion | flops 65536 | bytes 65536 | tf_op jit(solution)/shard_map/concatenate | solution.py:478
  2.8 1.0 %reshape.13.refs_0_ = bf16[6,64,256]{2,1,0:T(8,128)(2,1)S(1)} reshape(bf16[2,3,4,4,4,256]{5,4,3,2,1,0:T(4,128)(2,1)} %param.8) | data formatting | bytes 393216 | tf_op jit(solution)/shard_map/reshape | solution.py:474
  3.8 1.8 %squeeze_reshape.3.refs_7_ = bf16[2,256,1024]{2,1,0:T(8,128)(2,1)S(1)} reshape(bf16[1,2,256,4,256]{4,3,2,1,0:T(4,128)(2,1)} %param.11) | data formatting | bytes 2097152 | tf_op jit(solution)/shard_map/squeeze;reshape | solution.py:483
  5.6 0.0 copy-done.8
  5.6 0.0 copy-done.9
  5.6 0.0 copy-start.4
  5.6 0.7 %copy-done.4 = bf16[64,256]{1,0:T(8,128)(2,1)S(1)} copy-done((bf16[64,256]{1,0:T(8,128)(2,1)S(1)}, bf16[64,256]{1,0:T(8,128)(2,1)}, u32[]{:S(2)}) %copy-start.4) | copy-done | bytes 32792
  6.4 0.0 copy-start.5
  6.4 0.8 %copy-done.5 = s32[64,256]{1,0:T(8,128)S(1)} copy-done((s32[64,256]{1,0:T(8,128)S(1)}, s32[64,256]{1,0:T(8,128)}, u32[]{:S(2)}) %copy-start.5) | copy-done | bytes 65560
  7.2 0.0 copy-start.6
  7.2 0.8 %copy-done.6 = bf16[192,112]{1,0:T(8,128)(2,1)S(1)} copy-done((bf16[192,112]{1,0:T(8,128)(2,1)S(1)}, bf16[192,112]{1,0:T(8,128)(2,1)}, u32[]{:S(2)}) %copy-start.6) | copy-done | bytes 43032
  8.0 0.0 copy-start.7
  8.0 0.7 %copy-done.7 = bf16[96,64]{1,0:T(8,128)(2,1)S(1)} copy-done((bf16[96,64]{1,0:T(8,128)(2,1)S(1)}, bf16[96,64]{1,0:T(8,128)(2,1)}, u32[]{:S(2)}) %copy-start.7) | copy-done | bytes 12312
  8.7 35.4 %smear_project.1 = (bf16[6,64,256]{2,1,0:T(8,128)(2,1)S(1)}, bf16[4,256,256]{2,1,0:T(8,128)(2,1)S(1)}, bf16[1024,512]{1,0:T(8,128)(2,1)S(1)}, bf16[2048,512]{1,0:T(8,128)(2,1)S(1)}) custom-call(bf16[6,64,256]{2,1,0:T(8,128)(2,1)S(1)} %reshape.13.refs_0_, bf16[64,256]{1,0:T(8,128)(2,1)S(1)} %copy-done.4, s32[2,3]{1,0:T(2,128)S(1)} %copy-done.9, ...), custom_call_target="tpu_custom_call" | custom-call | tf_op jit(solution)/shard_map/smear_project/pallas_call | solution.py:386
  44.1 0.0 copy-start
  44.2 1.0 %copy-done = bf16[1024,512]{1,0:T(8,128)(2,1)} copy-done((bf16[1024,512]{1,0:T(8,128)(2,1)}, bf16[1024,512]{1,0:T(8,128)(2,1)S(1)}, u32[]{:S(2)}) %copy-start) | copy-done | bytes 1048600
  45.1 0.0 copy-start.2
  45.1 0.8 %copy-done.2 = bf16[4,256,256]{2,1,0:T(8,128)(2,1)} copy-done((bf16[4,256,256]{2,1,0:T(8,128)(2,1)}, bf16[4,256,256]{2,1,0:T(8,128)(2,1)S(1)}, u32[]{:S(2)}) %copy-start.2) | copy-done | bytes 524312
  45.9 0.7 %reshape.15 = bf16[2,3,4,4,4,256]{5,4,3,2,1,0:T(4,128)(2,1)} reshape(bf16[6,64,256]{2,1,0:T(8,128)(2,1)S(1)} %get-tuple-element.6) | data formatting | bytes 393216 | tf_op jit(solution)/shard_map/reshape | solution.py:491
  46.6 0.0 copy-start.1
  46.6 1.2 %copy-done.1 = bf16[1024,512]{1,0:T(8,128)(2,1)S(1)} copy-done((bf16[1024,512]{1,0:T(8,128)(2,1)S(1)}, bf16[1024,512]{1,0:T(8,128)(2,1)}, u32[]{:S(2)}) %copy-start.1) | copy-done | bytes 1048600
  47.9 0.0 copy-start.3
  47.9 1.0 %copy-done.3 = bf16[4,256,256]{2,1,0:T(8,128)(2,1)S(1)} copy-done((bf16[4,256,256]{2,1,0:T(8,128)(2,1)S(1)}, bf16[4,256,256]{2,1,0:T(8,128)(2,1)}, u32[]{:S(2)}) %copy-start.3) | copy-done | bytes 524312
  48.9 3.1 %sandwich.1 = bf16[2,2,256,256]{3,2,1,0:T(8,128)(2,1)} custom-call(bf16[4,256,256]{2,1,0:T(8,128)(2,1)S(1)} %copy-done.3, bf16[1024,512]{1,0:T(8,128)(2,1)S(1)} %copy-done.1, bf16[2048,512]{1,0:T(8,128)(2,1)S(1)} %get-tuple-element.9.rhs), custom_call_target="tpu_custom_call" | custom-call | tf_op jit(solution)/shard_map/sandwich/pallas_call | solution.py:435
  (1 shorter events, 0.0 us)
Async XLA Ops:
  0.6 5.0 %copy-start.8 = (bf16[48,64]{1,0:T(8,128)(2,1)S(1)}, bf16[48,64]{1,0:T(8,128)(2,1)}, u32[]{:S(2)}) copy-start(bf16[48,64]{1,0:T(8,128)(2,1)} %constant.13.clone.refs_5_) | copy-start | bytes 18436
  0.6 5.0 %copy-start.9 = (s32[2,3]{1,0:T(2,128)S(1)}, s32[2,3]{1,0:T(2,128)}, u32[]{:S(2)}) copy-start(s32[2,3]{1,0:T(2,128)} %refs_2_.1) | copy-start | bytes 76
  5.6 0.8 %copy-start.4 = (bf16[64,256]{1,0:T(8,128)(2,1)S(1)}, bf16[64,256]{1,0:T(8,128)(2,1)}, u32[]{:S(2)}) copy-start(bf16[64,256]{1,0:T(8,128)(2,1)} %pad_maximum_fusion.refs_1_) | copy-start | bytes 98308
  6.4 0.8 %copy-start.5 = (s32[64,256]{1,0:T(8,128)S(1)}, s32[64,256]{1,0:T(8,128)}, u32[]{:S(2)}) copy-start(s32[64,256]{1,0:T(8,128)} %constant.11.clone.refs_3_) | copy-start | bytes 196612
  7.2 0.8 %copy-start.6 = (bf16[192,112]{1,0:T(8,128)(2,1)S(1)}, bf16[192,112]{1,0:T(8,128)(2,1)}, u32[]{:S(2)}) copy-start(bf16[192,112]{1,0:T(8,128)(2,1)} %constant.14.clone.refs_6_) | copy-start | bytes 129028
  8.0 0.7 %copy-start.7 = (bf16[96,64]{1,0:T(8,128)(2,1)S(1)}, bf16[96,64]{1,0:T(8,128)(2,1)}, u32[]{:S(2)}) copy-start(bf16[96,64]{1,0:T(8,128)(2,1)} %constant.12.clone.refs_4_) | copy-start | bytes 36868
  44.1 1.0 %copy-start = (bf16[1024,512]{1,0:T(8,128)(2,1)}, bf16[1024,512]{1,0:T(8,128)(2,1)S(1)}, u32[]{:S(2)}) copy-start(bf16[1024,512]{1,0:T(8,128)(2,1)S(1)} %get-tuple-element.8.pt) | copy-start | bytes 3145732
  45.1 0.8 %copy-start.2 = (bf16[4,256,256]{2,1,0:T(8,128)(2,1)}, bf16[4,256,256]{2,1,0:T(8,128)(2,1)S(1)}, u32[]{:S(2)}) copy-start(bf16[4,256,256]{2,1,0:T(8,128)(2,1)S(1)} %get-tuple-element.7.ft_ref) | copy-start | bytes 1572868
  46.6 1.2 %copy-start.1 = (bf16[1024,512]{1,0:T(8,128)(2,1)S(1)}, bf16[1024,512]{1,0:T(8,128)(2,1)}, u32[]{:S(2)}) copy-start(bf16[1024,512]{1,0:T(8,128)(2,1)} %copy-done) | copy-start | bytes 3145732
  47.9 1.0 %copy-start.3 = (bf16[4,256,256]{2,1,0:T(8,128)(2,1)S(1)}, bf16[4,256,256]{2,1,0:T(8,128)(2,1)}, u32[]{:S(2)}) copy-start(bf16[4,256,256]{2,1,0:T(8,128)(2,1)} %copy-done.2) | copy-start | bytes 1572868

commit v3 on v2

--- a/solution.py
+++ b/solution.py
@@ -91,8 +91,8 @@
     cols = rhs_ref.shape[1] // 2
     spins = pt_ref.shape[0] // cols
     for s in range(spins):
-        real_p = p_ref[0, :, s * cols:(s + 1) * cols]
-        imag_p = p_ref[1, :, s * cols:(s + 1) * cols]
+        real_p = p_ref[0, :, s, :]
+        imag_p = p_ref[1, :, s, :]
         pt_ref[s * cols:(s + 1) * cols, 0:width] = jnp.transpose(real_p)
         pt_ref[s * cols:(s + 1) * cols, width:2 * width] = jnp.transpose(imag_p)
         r0 = s * 2 * width
@@ -103,9 +103,14 @@
 
 
 def main_kernel(plan, counts, scale, reduce_here, *refs):
-    (v_ref, lt_ref, mom_ref, code_ref, pick_ref, pickl_ref, below_ref, p_ref,
-     smeared_ref, out_ref, pt_ref, rhs_ref, tab, v1, v2, pk1, pk2, lk, lg, mh, ml, acc, half_out, half_in, plane_out, plane_in, z_out, z_in,
-     ssem, rsem) = refs
+    (mom_ref, *hbm) = refs[:8]
+    smeared_ref, result_ref, *local = refs[8:18]
+    v_ref, lt_ref, code_ref, pick_ref, pickl_ref, below_ref, p_ref, isem = local
+    (out_ref, pt_ref, rhs_ref, inner_ref, stage, tab, v1, v2, pk1, pk2, lk, lg, mh, ml, acc, half_out, half_in, plane_out, plane_in, z_out, z_in,
+     ssem, rsem) = refs[18:]
+    fetch = [pltpu.make_async_copy(hbm[k], local[k], isem.at[k]) for k in range(7)]
+    for c in fetch:
+        c.start()
     sites, cols, parts = plan.sites, plan.cols, 6
     me = [lax.axis_index(a) for a in AXES]
     nx, ny, nz = counts
@@ -142,7 +147,12 @@
             src_ref=src, dst_ref=dst, send_sem=ssem.at[k], recv_sem=rsem.at[k],
             device_id=device, device_id_type=MESH)
 
+    for c in fetch[:6]:
+        c.wait()
     pick = pick_ref[...]
+
+    def field_of(part):
+        return v_ref[part // 3, part % 3].reshape(sites, v_ref.shape[-1])
 
     def fill(buf, packed, part, value):
         buf[part, 0:sites, :] = value
@@ -152,14 +162,21 @@
     for buf in (v1, v2):
         if rest < cols:
             buf[:, rest:cols, :] = jnp.zeros((parts, cols - rest, buf.shape[2]), BF16)
-    lt = lt_ref[...]
+    stage[...] = jnp.zeros(stage.shape, F32)
+    for x in range(plan.dims[0]):
+        for y in range(plan.dims[1]):
+            s0 = (x * plan.dims[1] + y) * plan.dims[2]
+            stage[0:lt_ref.shape[0], s0:s0 + plan.dims[2]] = lt_ref[:, x, y, :]
+    turned = jnp.transpose(stage[...])[0:sites]
+    high = turned.astype(BF16)
+    lt = jnp.concatenate([high, (turned - high.astype(F32)).astype(BF16)], axis=1)
     lk[...] = dot(pickl_ref[...], lt).astype(BF16)
     lg[0:sites, :] = lt
     used_rows = sites + plan.ghosts
     if used_rows < plan.link_rows:
         lg[used_rows:, :] = jnp.zeros((plan.link_rows - used_rows, lg.shape[1]), BF16)
     for part in range(parts):
-        fill(v1, pk1, part, v_ref[part])
+        fill(v1, pk1, part, field_of(part))
     pl.semaphore_wait(barrier, len(greeted))
 
     sends = []
@@ -181,7 +198,7 @@
         return made
 
     halo1 = exchange(pk1, v1)
-    tab[...] = phase_table(plan, counts, me, mom_ref, out_ref.shape[0] // 2)
+    tab[...] = phase_table(plan, counts, me, mom_ref, mom_ref.shape[0])
     for c in links:
         c.wait_recv()
     sends += links
@@ -230,15 +247,15 @@
     for c in halo2:
         c.wait_recv()
     sends += halo2
-    vectors = v_ref[...].reshape(parts * sites, v_ref.shape[2]).astype(F32)
+    vectors = v1[:, 0:sites, :].reshape(parts * sites, v1.shape[2]).astype(F32)
     smeared = (2.0 * hop(v2) / 6.0 - vectors).astype(BF16)
     smeared_ref[...] = smeared.reshape(smeared_ref.shape)
     wide = smeared.astype(F32)
     rows = 3 * sites
     real_w, imag_w = wide[:rows], wide[rows:]
     left = jnp.transpose(wide).astype(BF16)
-    moms = out_ref.shape[0] // 2
-    width = v_ref.shape[2]
+    moms = mom_ref.shape[0]
+    width = v1.shape[2]
     for m in range(moms):
         cos_b = jnp.concatenate([tab[:, 2 * m:2 * m + 1]] * 3, axis=0)
         sin_b = jnp.concatenate([tab[:, 2 * m + 1:2 * m + 2]] * 3, axis=0)
@@ -248,8 +265,8 @@
         acc[moms + m] = dot(left, jnp.concatenate([imag_z, -real_z], axis=0)) * scale
 
     if not reduce_here:
-        prepare(p_ref, pt_ref, rhs_ref, width)
-        out_ref[...] = acc[...]
+        fetch[6].wait()
+        result_ref[...] = acc[...]
         for c in sends:
             c.wait_send()
         return
@@ -293,6 +310,7 @@
                 plane_in.at[r - 1, group[k]], plane_at(p)))
             row[-1].start()
         plane.append(row)
+    fetch[6].wait()
     prepare(p_ref, pt_ref, rhs_ref, width)
     sends += pair
     base = used[0]
@@ -358,18 +376,22 @@
         sends.append(c)
     for k in reversed(range(nz)):
         arrival(block(k, pl.ds(give, half)), pair[k])
+    spins, cols = p_ref.shape[2:]
+    sandwich_kernel(moms, spins, cols, out_ref, pt_ref, rhs_ref, result_ref, inner_ref)
     for c in sends:
         c.wait_send()
 
 
-def smear_and_project(plan, counts, scale, fields, links, momenta, rows, cols):
+def smear_and_project(plan, counts, scale, vectors, links, momenta, peram):
     moms = momenta.shape[0]
-    parts, sites, width = fields.shape
-    chunks = 2 * moms
+    sites, width = plan.sites, vectors.shape[-1]
+    parts, chunks = 6, 2 * moms
+    count, _, _, spins, cols = peram.shape
     nx, ny, nz = counts
     nq = max(nx * (ny // 2), 1)
     half = width // 2
-    reduce_here = ny % 2 == 0 and half % (16 * nq) == 0 and chunks % nz == 0 and nz > 1 and nq > 1
+    reduce_here = (count == 1 and ny % 2 == 0 and half % (16 * nq) == 0 and chunks % nz == 0
+                   and nz > 1 and nq > 1)
     vm = pltpu.VMEM
     if reduce_here:
         extra = [
@@ -379,21 +401,25 @@
             vm((nz - 1, chunks // nz, half // nq, width), BF16),
         ]
         copies = 3 + 12 + 2 * (nz + nz * (nq - 1) + (nz - 1))
+        result = jax.ShapeDtypeStruct((moms, 2, cols, cols), BF16)
     else:
         extra = [vm((8, 128), BF16)] * 6
         copies = 3 + 12
+        result = jax.ShapeDtypeStruct((chunks, width, width), F32)
     vmem = pl.BlockSpec(memory_space=pltpu.VMEM)
+    operands = [vectors, links, jnp.asarray(plan.code), jnp.asarray(plan.pick, BF16),
+                jnp.asarray(plan.pick_link, BF16), jnp.asarray(plan.below, BF16), peram[0]]
     return pl.pallas_call(
         functools.partial(main_kernel, plan, counts, scale, reduce_here),
-        out_shape=(
-            jax.ShapeDtypeStruct((parts, sites, width), BF16),
-            jax.ShapeDtypeStruct((chunks, width, width), BF16 if reduce_here else F32),
-            jax.ShapeDtypeStruct((rows.shape[2], 2 * width), BF16),
-            jax.ShapeDtypeStruct((rows.shape[2] // cols * 2 * width, 2 * cols), BF16),
-        ),
-        in_specs=[vmem, vmem, pl.BlockSpec(memory_space=pltpu.SMEM)] + [vmem] * 5,
-        out_specs=(vmem,) * 4,
+        out_shape=(jax.ShapeDtypeStruct(vectors.shape, BF16), result),
+        in_specs=[pl.BlockSpec(memory_space=pltpu.SMEM)]
+        + [pl.BlockSpec(memory_space=pl.ANY)] * 7,
+        out_specs=(vmem, vmem),
         scratch_shapes=[
+            *[vm(a.shape, a.dtype) for a in operands], pltpu.SemaphoreType.DMA((7,)),
+            vm((chunks, width, width), BF16), vm((spins * cols, 2 * width), BF16),
+            vm((spins * 2 * width, 2 * cols), BF16), vm((cols, spins * 2 * width), BF16),
+            vm((128, -(-sites // 128) * 128), F32),
             vm((sites, 128), F32),
             vm((parts, plan.cols, width), BF16), vm((parts, plan.cols, width), BF16),
             vm((parts, plan.halo, width), BF16), vm((parts, plan.halo, width), BF16),
@@ -405,10 +431,9 @@
             pltpu.SemaphoreType.DMA((copies,)), pltpu.SemaphoreType.DMA((copies,)),
         ],
         compiler_params=pltpu.CompilerParams(
-            collective_id=0, has_side_effects=True, vmem_limit_bytes=48 << 20),
+            collective_id=0, has_side_effects=True, vmem_limit_bytes=60 << 20),
         name="smear_project",
-    )(fields, links, momenta, jnp.asarray(plan.code), jnp.asarray(plan.pick, BF16),
-      jnp.asarray(plan.pick_link, BF16), jnp.asarray(plan.below, BF16), rows), reduce_here
+    )(momenta, *operands), reduce_here
 
 
 def sandwich_kernel(moms, spins, cols, ft_ref, pt, rhs, out_ref, inner):
@@ -445,9 +470,8 @@
     )(ft, pt, rhs)
 
 
-def prepare_one(rows, cols):
-    width = rows.shape[1]
-    spins = rows.shape[2] // cols
+def prepare_one(rows):
+    _, width, spins, cols = rows.shape
     vmem = pl.BlockSpec(memory_space=pltpu.VMEM)
 
     def kernel(p_ref, pt_ref, rhs_ref):
@@ -465,30 +489,52 @@
     )(rows)
 
 
+def settled(*arrays):
+    n = len(arrays)
+
+    def kernel(*refs):
+        held, sems = refs[2 * n:3 * n], refs[3 * n]
+        into = [pltpu.make_async_copy(refs[k], held[k], sems.at[k]) for k in range(n)]
+        back = [pltpu.make_async_copy(held[k], refs[n + k], sems.at[n + k]) for k in range(n)]
+        for c in into:
+            c.start()
+        for c, d in zip(into, back):
+            c.wait()
+            d.start()
+        for d in back:
+            d.wait()
+
+    return pl.pallas_call(
+        kernel,
+        out_shape=tuple(jax.ShapeDtypeStruct(a.shape, a.dtype) for a in arrays),
+        in_specs=[pl.BlockSpec(memory_space=pl.ANY)] * n,
+        out_specs=tuple(pl.BlockSpec(memory_space=pl.ANY) for _ in arrays),
+        scratch_shapes=[*[pltpu.VMEM(a.shape, a.dtype) for a in arrays],
+                        pltpu.SemaphoreType.DMA((2 * n,))],
+        compiler_params=pltpu.CompilerParams(vmem_limit_bytes=60 << 20),
+        name="settle",
+    )(*arrays)
+
+
 def per_device(counts, vectors, gauge_links, momenta, perambulator):
     dims = vectors.shape[2:5]
-    width = vectors.shape[5]
     plan = Plan(dims)
     sites = plan.sites
     cells = [dims[a] * counts[a] for a in range(3)]
-    fields = vectors.reshape(6, sites, width)
-    links = jnp.transpose(gauge_links.reshape(54, sites))
-    links = jnp.pad(links, ((0, 0), (0, 128 - 54)))
-    high = lax.reduce_precision(links, 8, 7)
-    links = jnp.concatenate([high.astype(BF16), (links - high).astype(BF16)], axis=1)
+    links = gauge_links.reshape((54,) + gauge_links.shape[4:])
     scale = 1.0 / math.sqrt(3.0 * cells[0] * cells[1] * cells[2])
+    (smeared, result), finished = smear_and_project(
+        plan, counts, scale, vectors, links, momenta, perambulator)
+    if finished:
+        smeared, result = settled(smeared, result)
+        return smeared, result[None]
+    ft = lax.psum(result, AXES).astype(BF16)
     count, _, _, spins, cols = perambulator.shape
-    rows = perambulator.reshape(count, 2, width, spins * cols)
-    (smeared, ft, pt, rhs), reduced = smear_and_project(
-        plan, counts, scale, fields, links, momenta, rows[0], cols)
-    if not reduced:
-        ft = lax.psum(ft, AXES).astype(BF16)
-    sandwich = [sandwich_of(ft, pt, rhs, spins, cols)]
-    for n in range(1, count):
-        pt, rhs = prepare_one(rows[n], cols)
+    sandwich = []
+    for n in range(count):
+        pt, rhs = prepare_one(perambulator[n])
         sandwich.append(sandwich_of(ft, pt, rhs, spins, cols))
-    sandwich = jnp.stack(sandwich)
-    return smeared.reshape(vectors.shape), sandwich
+    return smeared, jnp.stack(sandwich)
 
 
 def solution(mesh):

time: 52.5 us -> 41.6 us (0.79)
  the two profiles are of different devices: /device:TPU:0 before, /device:TPU:1 now
where the time goes in v3:
time: 41.6 us; the launch traced here: 41.4 us
  Pallas kernels  40.7 us (98%)
  between operations  0.64 us (2%)
    pallas_call x1, Pallas kernels, smear_and_project(): pl.pallas_call(functools.partial(main_kernel, plan, counts, scale, reduce...  38.8 us
    pallas_call x1, Pallas kernels, settled(): pl.pallas_call(kernel, out_shape=tuple((jax.ShapeDtypeStruct(a.shape, a.d...  1.98 us

profile of v3, /device:TPU:1, one launch (start us, length us, event | category | flops | bytes accessed | tf_op | source)
XLA Modules:
  0.0 41.4 jit_solution(7327426009460029116)
XLA Ops:
  0.6 38.8 %smear_project.1 = (bf16[2,3,4,4,4,256]{5,4,3,2,1,0:T(4,128)(2,1)}, bf16[2,2,256,256]{3,2,1,0:T(8,128)(2,1)}) custom-call(s32[2,3]{1,0:T(2,128)} %refs_0_.1, bf16[2,3,4,4,4,256]{5,4,3,2,1,0:T(4,128)(2,1)} %refs_1_.1, f32[54,4,4,4]{3,2,1,0:T(4,128)} %bitcast.4, s32[64,256]{1,0:T(8,128)} %constant.8.clone.refs_3_, bf16[96,64]{1,0:T(8,128)(2,1)} %constant.9.clone.refs_4_, ...), custom_call_target="tpu_custom_call" | custom-call | tf_op jit(solution)/shard_map/smear_project/pallas_call | solution.py:412
  39.4 2.0 %settle.1 = (bf16[2,3,4,4,4,256]{5,4,3,2,1,0:T(4,128)(2,1)}, bf16[2,2,256,256]{3,2,1,0:T(8,128)(2,1)}) custom-call(bf16[2,3,4,4,4,256]{5,4,3,2,1,0:T(4,128)(2,1)} %get-tuple-element.6.refs_0_, bf16[2,2,256,256]{3,2,1,0:T(8,128)(2,1)} %get-tuple-element.7.refs_1_), custom_call_target="tpu_custom_call" | custom-call | tf_op jit(solution)/shard_map/settle/pallas_call | solution.py:507
